TPU v7x, 32 devices: a whole 2x2x4 slice. The times are simulated.
32 devices in a mesh: traj: 2 (over x), dom: 16 (over z, y, core).
Axes of the slice: x: 2, y: 2, z: 4, core: 2. Of those that a mesh axis runs over, the one named last changes fastest.
Arguments:
- node_lat: bfloat16 [2, 4096, 512], P('traj', 'dom'), may hold values from -6 to 6
- edge_lat: bfloat16 [2, 8192, 512], P('traj', 'dom'), may hold values from -6 to 6
- grad_edge: bfloat16 [2, 8192, 512], P('traj', 'dom'), may hold values from -6 to 6
- grad_agg: bfloat16 [2, 4096, 512], P('traj', 'dom'), may hold values from -6 to 6
- weight_edge: bfloat16 [512, 512], replicated, may hold values from -0.15625 to 0.15625
- weight_send: bfloat16 [512, 512], replicated, may hold values from -0.15625 to 0.15625
- weight_recv: bfloat16 [512, 512], replicated, may hold values from -0.15625 to 0.15625
- weight_out: bfloat16 [512, 512], replicated, may hold values from -0.25 to 0.25
- edge_src: int32 [8192], P('dom'), may hold values from 0 to 767
- edge_recv_block: int32 [64], P('dom'), may hold values from 0 to 1
- edge_recv_node: int32 [8192], P('dom'), may hold values from 0 to 127
- send_blocks: int32 [64], P('dom'), may hold values from 0 to 1
Outputs:
- agg: bfloat16 [2, 4096, 512], P('traj', 'dom')
- grad_edge_lat: bfloat16 [2, 8192, 512], P('traj', 'dom')
- grad_node_lat: bfloat16 [2, 4096, 512], P('traj', 'dom')
- weight_grads: float32 [4, 512, 512], P(None, 'dom')
Inputs may be any that keep to these rules, and one draw needn't show every extreme that they name: edge_src // 128 is a slot below 6.
All inputs are finite; a program needn't handle non-finite values.
Results may differ from a plain program's by a relative error of at most 0.012.
Values may be sent and summed in bfloat16 or wider, within the bound.
No kernel may reach another device: no remote copies, remote signals or barrier semaphores. Data moves between devices by JAX's collectives and lax.ppermute only.
A program may use at most 64 MiB of HBM per device.

v0:
```python
import functools

import jax
import jax.numpy as jnp
from jax import lax
from jax.experimental import pallas as pl
from jax.experimental.pallas import tpu as pltpu
from jax.sharding import Mesh, PartitionSpec as P


LANES = 128
ROOM = 24 << 20
BF16 = jnp.bfloat16
F32 = jnp.float32
VMEM = pl.BlockSpec(memory_space=pltpu.VMEM)
SMEM = pl.BlockSpec(memory_space=pltpu.SMEM)


def dot(former, latter):
    return jnp.dot(former, latter, preferred_element_type=F32)


def dot_rows(former, latter):
    return lax.dot_general(former, latter, (((0,), (0,)), ((), ())), preferred_element_type=F32)


def dot_cols(former, latter):
    return lax.dot_general(former, latter, (((1,), (1,)), ((), ())), preferred_element_type=F32)


def near(array):
    return pltpu.with_memory_space_constraint(array, pltpu.VMEM)


def far(array):
    return pltpu.with_memory_space_constraint(array, pltpu.HBM)


def call(body, outs, ins, kept=True, scratch=()):
    fresh = pltpu.VMEM if kept else jax.ShapeDtypeStruct
    return pl.pallas_call(
        body,
        out_shape=[fresh(shape, kind) for shape, kind in outs],
        in_specs=ins,
        out_specs=[VMEM] * len(outs),
        scratch_shapes=scratch,
        compiler_params=pltpu.CompilerParams(vmem_limit_bytes=ROOM),
    )


def swap(array, axis):
    return lax.ppermute(array, axis, [(0, 1), (1, 0)])


def down_rows(row, count):
    return jnp.transpose(jnp.broadcast_to(row, (LANES, count)))


def onehot_cols(index_cols, first, blocks):
    lane = lax.broadcasted_iota(jnp.int32, index_cols.shape, 1)
    parts = [
        jnp.where(index_cols == lane + (first + LANES * block), 1.0, 0.0).astype(BF16)
        for block in range(blocks)
    ]
    return jnp.concatenate(parts, axis=1)


def onehot_rows(index_row, first, rows):
    node = lax.broadcasted_iota(jnp.int32, (rows, index_row.shape[1]), 0) + first
    return jnp.where(node == index_row, 1.0, 0.0).astype(BF16)


def receiver_row(recv_block, recv_node):
    edges = recv_node.shape[1]
    return jnp.concatenate(
        [
            recv_node[:, LANES * block : LANES * (block + 1)] + recv_block[block] * LANES
            for block in range(edges // LANES)
        ],
        axis=1,
    )


def pick_body(send_blocks, node_lat, *lent):
    for section, out in enumerate(lent):
        out[...] = node_lat[pl.ds(pl.multiple_of(send_blocks[section] * LANES, LANES), LANES), :]


def early_body(
    rounds, recv_block, send_blocks, edge_src, recv_node, node_lat, edge_lat, grad_edge, grad_agg, weight_edge,
    weight_recv, blocks_out, sender_out, receiver_out, edge_out, recv_out, send_out, hot_out,
    preact_out, grad_msg_out,
):
    nodes = node_lat.shape[0]
    edges = edge_lat.shape[0]
    row = receiver_row(recv_block, recv_node[...])
    receiver_out[...] = row
    blocks_out[...] = send_blocks[...]
    sender_out[...] = edge_src[...]
    edge_out[...] = edge_lat[...]
    receiver = down_rows(row, edges)
    sender = down_rows(edge_src[...], edges)
    hot_recv = onehot_cols(receiver, 0, nodes // LANES)
    recv_rows = dot(hot_recv, node_lat[...]).astype(BF16)
    recv_out[...] = recv_rows
    send_out[...] = dot(onehot_cols(sender, 0, nodes // LANES), node_lat[...]).astype(BF16)
    hot_out[...] = onehot_cols(sender, nodes, rounds)
    preact_out[...] = dot(edge_lat[...], weight_edge[...]) + dot(recv_rows, weight_recv[...])
    grad_msg_out[...] = grad_edge[...].astype(F32) + dot(hot_recv, grad_agg[...])


def place_of(split, dom_axes):
    domain = 0
    for axis in dom_axes:
        domain = domain * 2 + lax.axis_index(axis)
    return lax.axis_index(split[0]) if split else 0, domain


def store_rows(target, at, blocks):
    run = []
    for block in blocks:
        run.append(block)
        rows = sum(part.shape[0] for part in run)
        if rows % 16 == 0:
            whole = run[0] if len(run) == 1 else jnp.concatenate(run, axis=0)
            target[at : at + rows, :] = whole.astype(target.dtype)
            at += rows
            run = []


def give_rows(domains, where, sums, give_out, at=0):
    _, own = where()
    store_rows(give_out, at, [sums[own ^ (domain | 1)] for domain in domains])


def main_body(
    rounds, domains, where, send_own, hot, preact_own, grad_msg, weight_send, weight_out, *refs
):
    borrowed = refs[:rounds]
    send_out, grad_preact_out, message_out, sums_out, give_out, table = refs[rounds:]
    for section in range(rounds):
        table[LANES * section : LANES * (section + 1), :] = borrowed[section][...]
    send = (send_own[...].astype(F32) + dot(hot[...], table[...])).astype(BF16)
    send_out[...] = send
    preact = preact_own[...] + dot(send, weight_send[...])
    sigmoid = jax.nn.sigmoid(preact)
    hidden = (preact * sigmoid).astype(BF16)
    slope = sigmoid * (1.0 + preact * (1.0 - sigmoid))
    projected = dot(hidden, weight_out[...])
    centered = projected - jnp.mean(projected, axis=1, keepdims=True)
    inv_std = lax.rsqrt(jnp.mean(centered * centered, axis=1, keepdims=True) + 1e-05)
    normed = centered * inv_std
    message_out[...] = normed.astype(BF16)
    grad = grad_msg[...]
    grad_proj = inv_std * (
        grad
        - jnp.mean(grad, axis=1, keepdims=True)
        - normed * jnp.mean(grad * normed, axis=1, keepdims=True)
    )
    grad_proj = grad_proj.astype(BF16)
    grad_preact_out[...] = (dot_cols(grad_proj, weight_out[...]) * slope).astype(BF16)
    sums_out[...] = dot_rows(hidden, grad_proj).reshape(sums_out.shape)
    give_rows(domains, where, sums_out, give_out)


def grads_body(domains, where, *refs):
    *sums_outs, give_out = refs[-(len(refs) // 3) - 1 :]
    for which, sums_out in enumerate(sums_outs):
        former, latter = refs[2 * which : 2 * which + 2]
        sums_out[...] = dot_rows(former[...], latter[...]).reshape(sums_out.shape)
        rows = give_out.shape[0] // len(sums_outs)
        give_rows(domains, where, sums_out, give_out, which * rows)


def chip_body(plan, parts, where, places, *refs):
    keep_out, give_out = refs[-2:]
    sums, gots = refs[: len(places)], refs[len(places) : -2]
    count = len(sums) // parts
    part, own = where()
    half = len(plan) // 2

    def add(which, index, domain):
        share = sums[which].shape[1]
        holder, first = places[which]
        first += index * share
        start = first // 16 * 16
        got = gots[holder][start : start + max(share, 16), :].astype(F32)
        return sums[which][own ^ domain] + got[first - start : first - start + share]

    def write(this):
        for target, pieces in ((give_out, plan[half:]), (keep_out, plan[:half])):
            store_rows(
                target,
                0,
                [
                    add((this ^ flip) * count + which, index, domain)
                    for flip, index, domain in pieces
                    for which in range(count)
                ],
            )

    if parts == 1:
        write(0)
    else:
        for this in range(parts):
            pl.when(part == this)(functools.partial(write, this))


def sums_body(edge_src, receiver, grad_preact, own_out, recv_out, *back_out):
    nodes = own_out.shape[0]
    rounds = len(back_out)
    rows = grad_preact[...]
    slot_sums = dot(onehot_rows(edge_src[...], 0, nodes + rounds * LANES), rows)
    own_out[...] = slot_sums[:nodes]
    for section in range(rounds):
        first = nodes + LANES * section
        back_out[section][...] = slot_sums[first : first + LANES].astype(BF16)
    recv_out[...] = dot(onehot_rows(receiver[...], 0, nodes), rows)


def split_body(keep, got, keep_out, give_out):
    half = keep.shape[0] // 2
    for target, first in ((give_out, half), (keep_out, 0)):
        rows = slice(first, first + half)
        target[...] = (keep[rows, :] + got[rows, :].astype(F32)).astype(target.dtype)


def round_body(keep, got, out):
    out[...] = (keep[...] + got[...].astype(F32)).astype(BF16)


def finish_body(where, *refs):
    *parts, out = refs
    own, _ = where()
    if len(parts) == 4:
        whole, split, whole_got, split_got = parts
        take = split.shape[0]
        total = whole[...].astype(F32) + whole_got[...].astype(F32)
        for half in range(2):
            out[2 * half * take : (2 * half + 1) * take, :] = total[half * take : (half + 1) * take]
        for flip, part in enumerate((split, split_got)):
            first = pl.multiple_of((2 * (own ^ flip) + 1) * take, take)
            out[pl.ds(first, take), :] = part[...].astype(F32)
    else:
        take = parts[0].shape[0]
        for flip, part in enumerate(parts):
            first = pl.multiple_of((own ^ flip) * take, take)
            out[pl.ds(first, take), :] = part[...].astype(F32)


def edge_body(receiver, grad_preact, message, grad_edge, weight_edge, agg_out, edge_out):
    agg_out[...] = dot(onehot_rows(receiver[...], 0, agg_out.shape[0]), message[...]).astype(BF16)
    edge_out[...] = (
        grad_edge[...].astype(F32) + dot_cols(grad_preact[...], weight_edge[...])
    ).astype(BF16)


def dot_cols_split(former, latter):
    high = former.astype(BF16)
    low = (former - high.astype(F32)).astype(BF16)
    return dot_cols(high, latter) + dot_cols(low, latter)


def node_body(send_blocks, own_sums, recv_sums, weight_send, weight_recv, *refs):
    returned, out, total = refs[:-2], refs[-2], refs[-1]
    for first in range(0, out.shape[0], LANES):
        rows = slice(first, first + LANES)
        summed = own_sums[rows, :]
        for section, block in enumerate(returned):
            mine = send_blocks[:, section : section + 1] == first // LANES
            summed = summed + jnp.where(mine, block[...].astype(F32), 0.0)
        total[rows, :] = summed
    out[...] = (
        dot_cols_split(total[...], weight_send[...])
        + dot_cols_split(recv_sums[...], weight_recv[...])
    ).astype(BF16)


def layout(share, parts, tops):
    colours = 2 if parts == 2 and tops and share >= 16 else 1
    orders = [(["part"] if parts == 2 else []) + list(range(1, tops + 1))]
    if colours == 2:
        orders.insert(0, list(range(1, tops + 1)))
    domains = [index << 1 for index in range(2**tops)]
    plans = []
    for order in orders:
        pieces = []
        for index in range(2 ** len(order)):
            domain, flip = 0, 0
            for level, bit in enumerate(order):
                on = index >> (len(order) - 1 - level) & 1
                if bit == "part":
                    flip = on
                else:
                    domain |= on << bit
            pieces.append((flip, domain >> 1, domain))
        plans.append(pieces)
    return plans, orders, domains


def per_device(
    traj_axes, dom_axes, node_lat, edge_lat, grad_edge, grad_agg, weight_edge, weight_send,
    weight_recv, weight_out, edge_src, edge_recv_block, edge_recv_node, send_blocks,
):
    node_lat, edge_lat, grad_edge, grad_agg = node_lat[0], edge_lat[0], grad_edge[0], grad_agg[0]
    nodes, features = node_lat.shape
    edges = edge_lat.shape[0]
    rounds = send_blocks.shape[0]
    edge_src = edge_src.reshape(1, edges)
    recv_node = edge_recv_node.reshape(1, edges)
    bits = dom_axes[::-1]
    share = features // 2 ** len(bits)
    split = traj_axes[:1] if 2 * share >= 16 else ()
    plans, orders, domains = layout(share, 1 + len(split), len(bits) - 1)
    colours = len(orders)
    half = 2 * features
    wide = ((edges, features), BF16)
    wide_sum = ((edges, features), F32)
    node_sum = ((nodes, features), F32)
    block = ((LANES, features), BF16)
    where = functools.partial(place_of, split, dom_axes)

    lent = call(pick_body, [block] * rounds, [SMEM, VMEM])(
        far(send_blocks), far(node_lat)
    )
    borrowed = [swap(lent[section], bits[section]) for section in range(rounds)]
    blocks, sender, receiver, edge_rows, recv_rows, send_own, hot, preact_own, grad_msg = call(
        functools.partial(early_body, rounds),
        [((1, rounds), jnp.int32)] + [((1, edges), jnp.int32)] * 2 + [wide, wide, wide, ((edges, rounds * LANES), BF16), wide_sum, wide_sum],
        [SMEM] + [VMEM] * 9,
    )(
        *map(far, (edge_recv_block, send_blocks.reshape(1, rounds), edge_src, recv_node)),
        *map(far, (node_lat, edge_lat)),
        *map(far, (grad_edge, grad_agg, weight_edge, weight_recv)),
    )
    sum_rows = [
        ((2 ** len(bits), share, features), F32), ((share * len(domains), features), BF16)
    ]
    sums, gives = [None] * 4, [None] * 4
    send_rows, grad_preact, message, sums[3], gives[3] = call(
        functools.partial(main_body, rounds, domains, where),
        [wide] * 3 + sum_rows,
        [VMEM] * (6 + rounds),
        scratch=[pltpu.VMEM((rounds * LANES, features), BF16)],
    )(
        send_own, hot, preact_own, grad_msg, near(weight_send), near(weight_out),
        *map(near, borrowed),
    )
    factors = {0: (edge_rows, grad_preact), 1: (send_rows, grad_preact), 2: (recv_rows, grad_preact)}
    gave = {(3,): gives[3]}
    for group in ((1,), (0, 2)):
        shape, (give_shape, kind) = sum_rows
        *made, gave[group] = call(
            functools.partial(grads_body, domains, where),
            [shape] * len(group) + [((give_shape[0] * len(group), features), kind)],
            [VMEM] * (2 * len(group)),
        )(*sum((factors[which] for which in group), ()))
        for which, array in zip(group, made):
            sums[which] = array
    came = {group: near(swap(give, bits[0])) for group, give in gave.items()}
    flows, places = [], []
    for colour in range(colours):
        used = range(4)[colour::colours]
        groups = [group for group in came if set(group) & set(used)]
        rows = share * len(domains)
        places.append(
            [
                (holder, group.index(which) * rows)
                for which in used
                for holder, group in enumerate(groups)
                if which in group
            ]
        )
        flows.append([sums[which] for which in used] + [came[group] for group in groups])
    rows = half // colours

    own_sums, recv_sums, *back = call(
        sums_body, [node_sum, node_sum] + [block] * rounds, [VMEM] * 3
    )(sender, receiver, grad_preact)
    returned = [swap(back[section], bits[section]) for section in range(rounds)]

    def halves(rows):
        return [((rows, features), F32), ((rows, features), BF16)]

    depths = [len(order) for order in orders]
    for level in range(max(depths)):
        rows //= 2
        for colour, order in enumerate(orders):
            if level >= depths[colour]:
                continue
            if level:
                fold = call(split_body, halves(rows), [VMEM] * 2)
            else:
                parts = 2 if "part" in order else 1
                body = functools.partial(chip_body, plans[colour], parts, where, places[colour])
                fold = call(body, halves(rows), [VMEM] * len(flows[colour]))
            keep, give = fold(*flows[colour])
            axis = split[0] if order[level] == "part" else bits[order[level]]
            flows[colour] = (keep, near(swap(give, axis)))
    totals = []
    for flow in flows:
        sized = [((flow[0].shape[0], features), BF16)]
        (total,) = call(round_body, sized, [VMEM] * 2)(*flow)
        for axis in traj_axes[len(split) :]:
            (total,) = call(round_body, sized, [VMEM] * 2)(total, near(swap(total, axis)))
        totals.append(total)
    totals += [near(swap(total, axis)) for axis in split for total in totals]
    (weight_grads,) = call(
        functools.partial(finish_body, where),
        [((4 * share, features), F32)],
        [VMEM] * len(totals),
        kept=False,
    )(*totals)
    agg, grad_edges = call(
        edge_body, [((nodes, features), BF16), wide], [VMEM] * 5, kept=False
    )(receiver, grad_preact, message, near(grad_edge), near(weight_edge))
    (grad_nodes,) = call(
        node_body,
        [((nodes, features), BF16)],
        [VMEM] * (5 + rounds),
        kept=False,
        scratch=[pltpu.VMEM((nodes, features), F32)],
    )(
        blocks, own_sums, recv_sums, near(weight_send), near(weight_recv),
        *map(near, returned),
    )
    return agg[None], grad_edges[None], grad_nodes[None], weight_grads.reshape(4, share, features)


def solution(mesh):
    traj_axes = tuple(f"t{bit}" for bit in reversed(range(mesh.shape["traj"].bit_length() - 1)))
    dom_axes = tuple(f"d{bit}" for bit in reversed(range(mesh.shape["dom"].bit_length() - 1)))
    names = traj_axes + dom_axes
    bit_mesh = Mesh(mesh.devices.reshape((2,) * len(names)), names)
    rows = P(traj_axes, dom_axes, None)
    in_specs = (rows,) * 4 + (P(),) * 4 + (P(dom_axes),) * 4
    out_specs = (rows,) * 3 + (P(None, dom_axes, None),)

    def body(*arrays):
        return per_device(traj_axes, dom_axes, *arrays)

    return jax.shard_map(
        body, mesh=bit_mesh, in_specs=in_specs, out_specs=out_specs, check_vma=False
    )
```

profile of v0, /device:TPU:0, one launch (start us, length us, event | category | flops | bytes accessed | tf_op | source)
XLA Modules:
  0.0 57.3 jit_solution(12008355282721567464)
XLA Ops:
  0.6 1.0 %shard_map.148 = (bf16[128,512]{1,0:T(8,128)(2,1)S(1)}, bf16[128,512]{1,0:T(8,128)(2,1)S(1)}, bf16[128,512]{1,0:T(8,128)(2,1)S(1)}, bf16[128,512]{1,0:T(8,128)(2,1)S(1)}) custom-call(s32[4]{0:T(128)} %send_blocks.1, bf16[256,512]{1,0:T(8,128)(2,1)} %bitcast.13), custom_call_target="tpu_custom_call" | custom-call | tf_op jit(solution)/shard_map/pallas_call | solution.py:323
  2.2 2.6 %collective-permute-start.1 = (bf16[128,512]{1,0:T(8,128)(2,1)S(1)}, bf16[128,512]{1,0:T(8,128)(2,1)S(1)}, u32[]{:S(2)}, u32[]{:S(2)}) collective-permute-start(bf16[128,512]{1,0:T(8,128)(2,1)S(1)} %get-tuple-element.55), channel_id=1, source_target_pairs={{0,2},{2,0},{1,3},{3,1},{4,6},{6,4},{5,7},{7,5},{8,10},{10,8},{9,1... | collective-permute-start | bytes 393224 | tf_op jit(solution)/shard_map/ppermute | solution.py:52
  4.8 1.6 %collective-permute-start.2 = (bf16[128,512]{1,0:T(8,128)(2,1)S(1)}, bf16[128,512]{1,0:T(8,128)(2,1)S(1)}, u32[]{:S(2)}, u32[]{:S(2)}) collective-permute-start(bf16[128,512]{1,0:T(8,128)(2,1)S(1)} %get-tuple-element.56), channel_id=1, source_target_pairs={{0,4},{4,0},{1,5},{5,1},{2,6},{6,2},{3,7},{7,3},{8,12},{12,8},{9,1... | collective-permute-start | bytes 393224 | tf_op jit(solution)/shard_map/ppermute | solution.py:52
  6.4 2.6 %collective-permute-start.3 = (bf16[128,512]{1,0:T(8,128)(2,1)S(1)}, bf16[128,512]{1,0:T(8,128)(2,1)S(1)}, u32[]{:S(2)}, u32[]{:S(2)}) collective-permute-start(bf16[128,512]{1,0:T(8,128)(2,1)S(1)} %get-tuple-element.57), channel_id=1, source_target_pairs={{0,8},{8,0},{1,9},{9,1},{2,10},{10,2},{3,11},{11,3},{4,12},{12,4},... | collective-permute-start | bytes 393224 | tf_op jit(solution)/shard_map/ppermute | solution.py:52
  9.0 3.0 %shard_map.147 = (s32[1,4]{1,0:T(1,128)S(1)}, s32[1,512]{1,0:T(1,128)S(1)}, s32[1,512]{1,0:T(1,128)S(1)}, bf16[512,512]{1,0:T(8,128)(2,1)S(1)}, bf16[512,512]{1,...) custom-call(s32[4]{0:T(128)} %recv_block.1, ...), custom_call_target="tpu_custom_call" | custom-call | tf_op jit(solution)/shard_map/pallas_call | solution.py:327
  12.7 2.7 %collective-permute-done.3.refs_3_ = bf16[128,512]{1,0:T(8,128)(2,1)S(1)} collective-permute-done((bf16[128,512]{1,0:T(8,128)(2,1)S(1)}, bf16[128,512]{1,0:T(8,128)(2,1)S(1)}, u32[]{:S(2)}, u32[]{:S(2)}) %collective-permute-start.3) | collective-permute-done | bytes 131104 | tf_op jit(solution)/shard_map/ppermute | solution.py:52
  15.4 2.2 %shard_map.149 = (bf16[512,512]{1,0:T(8,128)(2,1)S(1)}, bf16[512,512]{1,0:T(8,128)(2,1)S(1)}, bf16[512,512]{1,0:T(8,128)(2,1)S(1)}, f32[16,32,512]{2,1,0:T(8,128)S(1)}, bf16[256,512]{1,0:T(8,128)(2,1)S(1)}) custom-call(bf16[512,512]{1,0:T(8,128)(2,1)S(1)} %get-tuple-element.50.send_own, bf16[512,512]{1,0:T(8,128)(2,1)S(1)} %get-tuple-element.51.hot, ...), custom_call_target="tpu_custom_call" | custom-call | tf_op jit(solution)/shard_map/pallas_call | solution.py:340
  17.6 0.8 %shard_map.153 = (f32[16,32,512]{2,1,0:T(8,128)S(1)}, f32[16,32,512]{2,1,0:T(8,128)S(1)}, bf16[512,512]{1,0:T(8,128)(2,1)S(1)}) custom-call(bf16[512,512]{1,0:T(8,128)(2,1)S(1)} %get-tuple-element.70.refs_0_, bf16[512,512]{1,0:T(8,128)(2,1)S(1)} %get-tuple-element.58.grad_preact.refs_1_.refs_3_, bf16[512,512]{1,0:T(8,128)(2,1)S(1)} %get-tuple-element.71.refs_2_, ...), custom_call_target="tpu_custom_call" | custom-call | tf_op jit(solution)/shard_map/pallas_call | solution.py:353
  19.6 1.1 %collective-permute-done.12.refs_2_ = bf16[256,512]{1,0:T(8,128)(2,1)S(1)} collective-permute-done((bf16[256,512]{1,0:T(8,128)(2,1)S(1)}, bf16[256,512]{1,0:T(8,128)(2,1)S(1)}, u32[]{:S(2)}, u32[]{:S(2)}) %collective-permute-start.12) | collective-permute-done | bytes 262176 | tf_op jit(solution)/shard_map/ppermute | solution.py:52
  21.2 1.5 %collective-permute-start.14 = (bf16[256,512]{1,0:T(8,128)(2,1)S(1)}, bf16[256,512]{1,0:T(8,128)(2,1)S(1)}, u32[]{:S(2)}, u32[]{:S(2)}) collective-permute-start(bf16[256,512]{1,0:T(8,128)(2,1)S(1)} %get-tuple-element.87), channel_id=1, source_target_pairs={{0,16},{16,0},{1,17},{17,1},{2,18},{18,2},{3,19},{19,3},{4,20},{20... | collective-permute-start | bytes 786440 | tf_op jit(solution)/shard_map/ppermute | solution.py:52
  23.4 6.2 %collective-permute-done.14.got = bf16[256,512]{1,0:T(8,128)(2,1)S(1)} collective-permute-done((bf16[256,512]{1,0:T(8,128)(2,1)S(1)}, bf16[256,512]{1,0:T(8,128)(2,1)S(1)}, u32[]{:S(2)}, u32[]{:S(2)}) %collective-permute-start.14) | collective-permute-done | bytes 262176 | tf_op jit(solution)/shard_map/ppermute | solution.py:52
  30.2 0.8 %collective-permute-done.9.got = bf16[256,512]{1,0:T(8,128)(2,1)S(1)} collective-permute-done((bf16[256,512]{1,0:T(8,128)(2,1)S(1)}, bf16[256,512]{1,0:T(8,128)(2,1)S(1)}, u32[]{:S(2)}, u32[]{:S(2)}) %collective-permute-start.9) | collective-permute-done | bytes 262176 | tf_op jit(solution)/shard_map/ppermute | solution.py:52
  31.5 3.1 %collective-permute-done.15.got = bf16[128,512]{1,0:T(8,128)(2,1)S(1)} collective-permute-done((bf16[128,512]{1,0:T(8,128)(2,1)S(1)}, bf16[128,512]{1,0:T(8,128)(2,1)S(1)}, u32[]{:S(2)}, u32[]{:S(2)}) %collective-permute-start.15) | collective-permute-done | bytes 131104 | tf_op jit(solution)/shard_map/ppermute | solution.py:52
  35.2 0.7 %shard_map.151 = (f32[256,512]{1,0:T(8,128)S(1)}, f32[256,512]{1,0:T(8,128)S(1)}, bf16[128,512]{1,0:T(8,128)(2,1)S(1)}, bf16[128,512]{1,0:T(8,128)(2,1)S(1)}, bf...) custom-call(s32[1,512]{1,0:T(1,128)S(1)} %get-tuple-element.63.edge_src, ...), custom_call_target="tpu_custom_call" | custom-call | tf_op jit(solution)/shard_map/pallas_call | solution.py:377
  35.9 0.7 %collective-permute-done.10.got = bf16[128,512]{1,0:T(8,128)(2,1)S(1)} collective-permute-done((bf16[128,512]{1,0:T(8,128)(2,1)S(1)}, bf16[128,512]{1,0:T(8,128)(2,1)S(1)}, u32[]{:S(2)}, u32[]{:S(2)}) %collective-permute-start.10) | collective-permute-done | bytes 131104 | tf_op jit(solution)/shard_map/ppermute | solution.py:52
  36.6 2.0 %collective-permute-start.11 = (bf16[64,512]{1,0:T(8,128)(2,1)S(1)}, bf16[64,512]{1,0:T(8,128)(2,1)S(1)}, u32[]{:S(2)}, u32[]{:S(2)}) collective-permute-start(bf16[64,512]{1,0:T(8,128)(2,1)S(1)} %get-tuple-element.80), channel_id=1, source_target_pairs={{0,8},{8,0},{1,9},{9,1},{2,10},{10,2},{3,11},{11,3},{4,12},{12,4},... | collective-permute-start | bytes 196616 | tf_op jit(solution)/shard_map/ppermute | solution.py:52
  39.1 1.5 %collective-permute-start.6 = (bf16[128,512]{1,0:T(8,128)(2,1)S(1)}, bf16[128,512]{1,0:T(8,128)(2,1)S(1)}, u32[]{:S(2)}, u32[]{:S(2)}) collective-permute-start(bf16[128,512]{1,0:T(8,128)(2,1)S(1)} %get-tuple-element.68), channel_id=1, source_target_pairs={{0,4},{4,0},{1,5},{5,1},{2,6},{6,2},{3,7},{7,3},{8,12},{12,8},{9,1... | collective-permute-start | bytes 393224 | tf_op jit(solution)/shard_map/ppermute | solution.py:52
  41.1 1.6 %collective-permute-done.11.got = bf16[64,512]{1,0:T(8,128)(2,1)S(1)} collective-permute-done((bf16[64,512]{1,0:T(8,128)(2,1)S(1)}, bf16[64,512]{1,0:T(8,128)(2,1)S(1)}, u32[]{:S(2)}, u32[]{:S(2)}) %collective-permute-start.11) | collective-permute-done | bytes 65568 | tf_op jit(solution)/shard_map/ppermute | solution.py:52
  42.7 1.2 %collective-permute-start.17 = (bf16[32,512]{1,0:T(8,128)(2,1)S(1)}, bf16[32,512]{1,0:T(8,128)(2,1)S(1)}, u32[]{:S(2)}, u32[]{:S(2)}) collective-permute-start(bf16[32,512]{1,0:T(8,128)(2,1)S(1)} %get-tuple-element.93), channel_id=1, source_target_pairs={{0,8},{8,0},{1,9},{9,1},{2,10},{10,2},{3,11},{11,3},{4,12},{12,4},... | collective-permute-start | bytes 98312 | tf_op jit(solution)/shard_map/ppermute | solution.py:52
  43.9 7.2 %collective-permute-done.17.got = bf16[32,512]{1,0:T(8,128)(2,1)S(1)} collective-permute-done((bf16[32,512]{1,0:T(8,128)(2,1)S(1)}, bf16[32,512]{1,0:T(8,128)(2,1)S(1)}, u32[]{:S(2)}, u32[]{:S(2)}) %collective-permute-start.17) | collective-permute-done | bytes 32800 | tf_op jit(solution)/shard_map/ppermute | solution.py:52
  51.1 1.5 %collective-permute-start.18 = (bf16[64,512]{1,0:T(8,128)(2,1)S(1)}, bf16[64,512]{1,0:T(8,128)(2,1)S(1)}, u32[]{:S(2)}, u32[]{:S(2)}) collective-permute-start(bf16[64,512]{1,0:T(8,128)(2,1)S(1)} %shard_map.157.refs_0_), channel_id=1, source_target_pairs={{0,16},{16,0},{1,17},{17,1},{2,18},{18,2},{3,19},{19,3},{4,20},{20... | collective-permute-start | bytes 196616 | tf_op jit(solution)/shard_map/ppermute | solution.py:52
  53.2 1.4 %shard_map.150 = (bf16[256,512]{1,0:T(8,128)(2,1)}, bf16[512,512]{1,0:T(8,128)(2,1)}) custom-call(s32[1,512]{1,0:T(1,128)S(1)} %get-tuple-element.49.receiver, bf16[512,512]{1,0:T(8,128)(2,1)S(1)} %get-tuple-element.58.grad_preact.refs_1_.refs_3_, bf16[512,512]{1,0:T(8,128)(2,1)S(1)} %get-tuple-element.59.message, bf16[512,512]{1,0:T(8,128)(2,1)S(1)} %bitcast.12, ...), custom_call_target="tpu_custom_call" | custom-call | tf_op jit(solution)/shard_map/pallas_call | solution.py:414
  54.6 1.6 %shard_map.152 = bf16[256,512]{1,0:T(8,128)(2,1)} custom-call(s32[1,4]{1,0:T(1,128)S(1)} %get-tuple-element.62.send_blocks, f32[256,512]{1,0:T(8,128)S(1)} %get-tuple-element.64.own_sums, f32[256,512]{1,0:T(8,128)S(1)} %get-tuple-element.65.recv_sums, bf16[512,512]{1,0:T(8,128)(2,1)S(1)} %copy-done.3, bf16[512,512]{1,0:T(8,128)(2,1)S(1)} %copy-done.2, ...), custom_call_target="tpu_custom_call" | custom-call | tf_op jit(solution)/shard_map/pallas_call | solution.py:417
  56.6 0.7 %shard_map.164 = f32[128,512]{1,0:T(8,128)} custom-call(bf16[64,512]{1,0:T(8,128)(2,1)S(1)} %shard_map.157.refs_0_, bf16[32,512]{1,0:T(8,128)(2,1)S(1)} %shard_map.163.refs_1_, bf16[64,512]{1,0:T(8,128)(2,1)S(1)} %collective-permute-done.18.refs_2_, bf16[32,512]{1,0:T(8,128)(2,1)S(1)} %collective-permute-done.19.refs_3_), custom_call_target="tpu_custom_call" | custom-call | tf_op jit(solution)/shard_map/pallas_call | solution.py:408
  (44 shorter events, 7.2 us)
Async XLA Ops:
  1.6 10.4 %collective-permute-start = (bf16[128,512]{1,0:T(8,128)(2,1)S(1)}, bf16[128,512]{1,0:T(8,128)(2,1)S(1)}, u32[]{:S(2)}, u32[]{:S(2)}) collective-permute-start(bf16[128,512]{1,0:T(8,128)(2,1)S(1)} %get-tuple-element.54), channel_id=1, source_target_pairs={{0,1},{1,0},{2,3},{3,2},{4,5},{5,4},{6,7},{7,6},{8,9},{9,8},{10,11... | collective-permute-start | bytes 393224 | tf_op jit(solution)/shard_map/ppermute | solution.py:52
  2.2 9.8 %collective-permute-start.1 = (bf16[128,512]{1,0:T(8,128)(2,1)S(1)}, bf16[128,512]{1,0:T(8,128)(2,1)S(1)}, u32[]{:S(2)}, u32[]{:S(2)}) collective-permute-start(bf16[128,512]{1,0:T(8,128)(2,1)S(1)} %get-tuple-element.55), channel_id=1, source_target_pairs={{0,2},{2,0},{1,3},{3,1},{4,6},{6,4},{5,7},{7,5},{8,10},{10,8},{9,1... | collective-permute-start | bytes 393224 | tf_op jit(solution)/shard_map/ppermute | solution.py:52
  4.8 7.9 %collective-permute-start.2 = (bf16[128,512]{1,0:T(8,128)(2,1)S(1)}, bf16[128,512]{1,0:T(8,128)(2,1)S(1)}, u32[]{:S(2)}, u32[]{:S(2)}) collective-permute-start(bf16[128,512]{1,0:T(8,128)(2,1)S(1)} %get-tuple-element.56), channel_id=1, source_target_pairs={{0,4},{4,0},{1,5},{5,1},{2,6},{6,2},{3,7},{7,3},{8,12},{12,8},{9,1... | collective-permute-start | bytes 393224 | tf_op jit(solution)/shard_map/ppermute | solution.py:52
  6.4 9.0 %collective-permute-start.3 = (bf16[128,512]{1,0:T(8,128)(2,1)S(1)}, bf16[128,512]{1,0:T(8,128)(2,1)S(1)}, u32[]{:S(2)}, u32[]{:S(2)}) collective-permute-start(bf16[128,512]{1,0:T(8,128)(2,1)S(1)} %get-tuple-element.57), channel_id=1, source_target_pairs={{0,8},{8,0},{1,9},{9,1},{2,10},{10,2},{3,11},{11,3},{4,12},{12,4},... | collective-permute-start | bytes 393224 | tf_op jit(solution)/shard_map/ppermute | solution.py:52
  8.9 6.4 %copy-start.3 = (bf16[512,512]{1,0:T(8,128)(2,1)S(1)}, bf16[512,512]{1,0:T(8,128)(2,1)}, u32[]{:S(2)}) copy-start(bf16[512,512]{1,0:T(8,128)(2,1)} %weight_send.3) | copy-start | bytes 1572868
  8.9 6.4 %copy-start.4 = (bf16[512,512]{1,0:T(8,128)(2,1)S(1)}, bf16[512,512]{1,0:T(8,128)(2,1)}, u32[]{:S(2)}) copy-start(bf16[512,512]{1,0:T(8,128)(2,1)} %weight_out.1) | copy-start | bytes 1572868
  18.4 4.4 %collective-permute-start.8 = (bf16[512,512]{1,0:T(8,128)(2,1)S(1)}, bf16[512,512]{1,0:T(8,128)(2,1)S(1)}, u32[]{:S(2)}, u32[]{:S(2)}) collective-permute-start(bf16[512,512]{1,0:T(8,128)(2,1)S(1)} %get-tuple-element.74), channel_id=1, source_target_pairs={{0,1},{1,0},{2,3},{3,2},{4,5},{5,4},{6,7},{7,6},{8,9},{9,8},{10,11... | collective-permute-start | bytes 1572872 | tf_op jit(solution)/shard_map/ppermute | solution.py:52
  18.4 2.3 %collective-permute-start.12 = (bf16[256,512]{1,0:T(8,128)(2,1)S(1)}, bf16[256,512]{1,0:T(8,128)(2,1)S(1)}, u32[]{:S(2)}, u32[]{:S(2)}) collective-permute-start(bf16[256,512]{1,0:T(8,128)(2,1)S(1)} %get-tuple-element.84), channel_id=1, source_target_pairs={{0,1},{1,0},{2,3},{3,2},{4,5},{5,4},{6,7},{7,6},{8,9},{9,8},{10,11... | collective-permute-start | bytes 786440 | tf_op jit(solution)/shard_map/ppermute | solution.py:52
  19.4 1.7 %collective-permute-start.13 = (bf16[256,512]{1,0:T(8,128)(2,1)S(1)}, bf16[256,512]{1,0:T(8,128)(2,1)S(1)}, u32[]{:S(2)}, u32[]{:S(2)}) collective-permute-start(bf16[256,512]{1,0:T(8,128)(2,1)S(1)} %get-tuple-element.85), channel_id=1, source_target_pairs={{0,1},{1,0},{2,3},{3,2},{4,5},{5,4},{6,7},{7,6},{8,9},{9,8},{10,11... | collective-permute-start | bytes 786440 | tf_op jit(solution)/shard_map/ppermute | solution.py:52
  21.2 8.4 %collective-permute-start.14 = (bf16[256,512]{1,0:T(8,128)(2,1)S(1)}, bf16[256,512]{1,0:T(8,128)(2,1)S(1)}, u32[]{:S(2)}, u32[]{:S(2)}) collective-permute-start(bf16[256,512]{1,0:T(8,128)(2,1)S(1)} %get-tuple-element.87), channel_id=1, source_target_pairs={{0,16},{16,0},{1,17},{17,1},{2,18},{18,2},{3,19},{19,3},{4,20},{20... | collective-permute-start | bytes 786440 | tf_op jit(solution)/shard_map/ppermute | solution.py:52
  22.8 8.1 %collective-permute-start.9 = (bf16[256,512]{1,0:T(8,128)(2,1)S(1)}, bf16[256,512]{1,0:T(8,128)(2,1)S(1)}, u32[]{:S(2)}, u32[]{:S(2)}) collective-permute-start(bf16[256,512]{1,0:T(8,128)(2,1)S(1)} %get-tuple-element.76), channel_id=1, source_target_pairs={{0,2},{2,0},{1,3},{3,1},{4,6},{6,4},{5,7},{7,5},{8,10},{10,8},{9,1... | collective-permute-start | bytes 786440 | tf_op jit(solution)/shard_map/ppermute | solution.py:52
  29.6 5.0 %collective-permute-start.15 = (bf16[128,512]{1,0:T(8,128)(2,1)S(1)}, bf16[128,512]{1,0:T(8,128)(2,1)S(1)}, u32[]{:S(2)}, u32[]{:S(2)}) collective-permute-start(bf16[128,512]{1,0:T(8,128)(2,1)S(1)} %get-tuple-element.89), channel_id=1, source_target_pairs={{0,2},{2,0},{1,3},{3,1},{4,6},{6,4},{5,7},{7,5},{8,10},{10,8},{9,1... | collective-permute-start | bytes 393224 | tf_op jit(solution)/shard_map/ppermute | solution.py:52
  31.0 5.6 %collective-permute-start.10 = (bf16[128,512]{1,0:T(8,128)(2,1)S(1)}, bf16[128,512]{1,0:T(8,128)(2,1)S(1)}, u32[]{:S(2)}, u32[]{:S(2)}) collective-permute-start(bf16[128,512]{1,0:T(8,128)(2,1)S(1)} %get-tuple-element.78), channel_id=1, source_target_pairs={{0,4},{4,0},{1,5},{5,1},{2,6},{6,2},{3,7},{7,3},{8,12},{12,8},{9,1... | collective-permute-start | bytes 393224 | tf_op jit(solution)/shard_map/ppermute | solution.py:52
  34.7 6.0 %collective-permute-start.16 = (bf16[64,512]{1,0:T(8,128)(2,1)S(1)}, bf16[64,512]{1,0:T(8,128)(2,1)S(1)}, u32[]{:S(2)}, u32[]{:S(2)}) collective-permute-start(bf16[64,512]{1,0:T(8,128)(2,1)S(1)} %get-tuple-element.91), channel_id=1, source_target_pairs={{0,4},{4,0},{1,5},{5,1},{2,6},{6,2},{3,7},{7,3},{8,12},{12,8},{9,1... | collective-permute-start | bytes 196616 | tf_op jit(solution)/shard_map/ppermute | solution.py:52
  35.2 18.0 %copy-start.1 = (bf16[512,512]{1,0:T(8,128)(2,1)S(1)}, bf16[512,512]{1,0:T(8,128)(2,1)}, u32[]{:S(2)}) copy-start(bf16[512,512]{1,0:T(8,128)(2,1)} %weight_edge.3) | copy-start | bytes 1572868
  35.9 17.3 %copy-start = (bf16[1,512,512]{2,1,0:T(8,128)(2,1)S(1)}, bf16[1,512,512]{2,1,0:T(8,128)(2,1)}, u32[]{:S(2)}) copy-start(bf16[1,512,512]{2,1,0:T(8,128)(2,1)} %param.14) | copy-start | bytes 1572868
  36.6 6.0 %collective-permute-start.11 = (bf16[64,512]{1,0:T(8,128)(2,1)S(1)}, bf16[64,512]{1,0:T(8,128)(2,1)S(1)}, u32[]{:S(2)}, u32[]{:S(2)}) collective-permute-start(bf16[64,512]{1,0:T(8,128)(2,1)S(1)} %get-tuple-element.80), channel_id=1, source_target_pairs={{0,8},{8,0},{1,9},{9,1},{2,10},{10,2},{3,11},{11,3},{4,12},{12,4},... | collective-permute-start | bytes 196616 | tf_op jit(solution)/shard_map/ppermute | solution.py:52
  38.6 14.0 %collective-permute-start.4 = (bf16[128,512]{1,0:T(8,128)(2,1)S(1)}, bf16[128,512]{1,0:T(8,128)(2,1)S(1)}, u32[]{:S(2)}, u32[]{:S(2)}) collective-permute-start(bf16[128,512]{1,0:T(8,128)(2,1)S(1)} %get-tuple-element.66), channel_id=1, source_target_pairs={{0,1},{1,0},{2,3},{3,2},{4,5},{5,4},{6,7},{7,6},{8,9},{9,8},{10,11... | collective-permute-start | bytes 393224 | tf_op jit(solution)/shard_map/ppermute | solution.py:52
  38.6 16.0 %collective-permute-start.5 = (bf16[128,512]{1,0:T(8,128)(2,1)S(1)}, bf16[128,512]{1,0:T(8,128)(2,1)S(1)}, u32[]{:S(2)}, u32[]{:S(2)}) collective-permute-start(bf16[128,512]{1,0:T(8,128)(2,1)S(1)} %get-tuple-element.67), channel_id=1, source_target_pairs={{0,2},{2,0},{1,3},{3,1},{4,6},{6,4},{5,7},{7,5},{8,10},{10,8},{9,1... | collective-permute-start | bytes 393224 | tf_op jit(solution)/shard_map/ppermute | solution.py:52
  39.1 15.5 %collective-permute-start.6 = (bf16[128,512]{1,0:T(8,128)(2,1)S(1)}, bf16[128,512]{1,0:T(8,128)(2,1)S(1)}, u32[]{:S(2)}, u32[]{:S(2)}) collective-permute-start(bf16[128,512]{1,0:T(8,128)(2,1)S(1)} %get-tuple-element.68), channel_id=1, source_target_pairs={{0,4},{4,0},{1,5},{5,1},{2,6},{6,2},{3,7},{7,3},{8,12},{12,8},{9,1... | collective-permute-start | bytes 393224 | tf_op jit(solution)/shard_map/ppermute | solution.py:52
  40.6 14.0 %collective-permute-start.7 = (bf16[128,512]{1,0:T(8,128)(2,1)S(1)}, bf16[128,512]{1,0:T(8,128)(2,1)S(1)}, u32[]{:S(2)}, u32[]{:S(2)}) collective-permute-start(bf16[128,512]{1,0:T(8,128)(2,1)S(1)} %get-tuple-element.69), channel_id=1, source_target_pairs={{0,8},{8,0},{1,9},{9,1},{2,10},{10,2},{3,11},{11,3},{4,12},{12,4},... | collective-permute-start | bytes 393224 | tf_op jit(solution)/shard_map/ppermute | solution.py:52
  42.7 8.4 %collective-permute-start.17 = (bf16[32,512]{1,0:T(8,128)(2,1)S(1)}, bf16[32,512]{1,0:T(8,128)(2,1)S(1)}, u32[]{:S(2)}, u32[]{:S(2)}) collective-permute-start(bf16[32,512]{1,0:T(8,128)(2,1)S(1)} %get-tuple-element.93), channel_id=1, source_target_pairs={{0,8},{8,0},{1,9},{9,1},{2,10},{10,2},{3,11},{11,3},{4,12},{12,4},... | collective-permute-start | bytes 98312 | tf_op jit(solution)/shard_map/ppermute | solution.py:52
  51.1 5.5 %collective-permute-start.18 = (bf16[64,512]{1,0:T(8,128)(2,1)S(1)}, bf16[64,512]{1,0:T(8,128)(2,1)S(1)}, u32[]{:S(2)}, u32[]{:S(2)}) collective-permute-start(bf16[64,512]{1,0:T(8,128)(2,1)S(1)} %shard_map.157.refs_0_), channel_id=1, source_target_pairs={{0,16},{16,0},{1,17},{17,1},{2,18},{18,2},{3,19},{19,3},{4,20},{20... | collective-permute-start | bytes 196616 | tf_op jit(solution)/shard_map/ppermute | solution.py:52
  52.6 4.0 %collective-permute-start.19 = (bf16[32,512]{1,0:T(8,128)(2,1)S(1)}, bf16[32,512]{1,0:T(8,128)(2,1)S(1)}, u32[]{:S(2)}, u32[]{:S(2)}) collective-permute-start(bf16[32,512]{1,0:T(8,128)(2,1)S(1)} %shard_map.163.refs_1_), channel_id=1, source_target_pairs={{0,16},{16,0},{1,17},{17,1},{2,18},{18,2},{3,19},{19,3},{4,20},{20... | collective-permute-start | bytes 98312 | tf_op jit(solution)/shard_map/ppermute | solution.py:52
  (1 other events, 1.4 us)
where the time goes:
time: 57.5 us; the launch traced here: 57.3 us
  waiting for transfers between devices  24.9 us (43%)
  starting transfers between devices  19.4 us (34%)
  Pallas kernels  12.2 us (21%)
  between operations  0.79 us (1%)
    ppermute x20, waiting for transfers between devices, swap(): return lax.ppermute(array, axis, [(0, 1), (1, 0)])  24.9 us
    ppermute x20, starting transfers between devices, swap(): return lax.ppermute(array, axis, [(0, 1), (1, 0)])  19.4 us
    pallas_call x1, Pallas kernels, per_device(): call(functools.partial(early_body, rounds), [((1, rounds), jnp.int32)] +...  3.04 us
    pallas_call x1, Pallas kernels, per_device(): call(functools.partial(main_body, rounds, domains, where), [wide] * 3 + s...  2.18 us
    pallas_call x1, Pallas kernels, per_device(): call(node_body, [((nodes, features), BF16)], [VMEM] * (5 + rounds), kept=...  1.59 us
    pallas_call x1, Pallas kernels, per_device(): call(edge_body, [((nodes, features), BF16), wide], [VMEM] * 5, kept=False)  1.37 us
    pallas_call x2, Pallas kernels, per_device(): call(functools.partial(grads_body, domains, where), [shape] * len(group)...  1.25 us
  transfers between devices with their start and end apart: 20, of which 11 were waited for; matrix products, arithmetic and copies ran while one was open for 0% of the time, Pallas kernels for 13%

commit v1 on v0

--- a/solution.py
+++ b/solution.py
@@ -106,7 +106,8 @@
     send_out[...] = dot(onehot_cols(sender, 0, nodes // LANES), node_lat[...]).astype(BF16)
     hot_out[...] = onehot_cols(sender, nodes, rounds)
     preact_out[...] = dot(edge_lat[...], weight_edge[...]) + dot(recv_rows, weight_recv[...])
-    grad_msg_out[...] = grad_edge[...].astype(F32) + dot(hot_recv, grad_agg[...])
+    grad_msg = grad_edge[...].astype(F32) + dot(hot_recv, grad_agg[...])
+    grad_msg_out[...] = grad_msg - jnp.mean(grad_msg, axis=1, keepdims=True)
 
 
 def place_of(split, dom_axes):
@@ -152,11 +153,7 @@
     normed = centered * inv_std
     message_out[...] = normed.astype(BF16)
     grad = grad_msg[...]
-    grad_proj = inv_std * (
-        grad
-        - jnp.mean(grad, axis=1, keepdims=True)
-        - normed * jnp.mean(grad * normed, axis=1, keepdims=True)
-    )
+    grad_proj = inv_std * (grad - normed * jnp.mean(grad * normed, axis=1, keepdims=True))
     grad_proj = grad_proj.astype(BF16)
     grad_preact_out[...] = (dot_cols(grad_proj, weight_out[...]) * slope).astype(BF16)
     sums_out[...] = dot_rows(hidden, grad_proj).reshape(sums_out.shape)

time: 57.5 us -> 57.4 us (level)
  no operation moved by 1% of the time
where the time goes in v1:
time: 57.4 us; the launch traced here: 57.3 us
  waiting for transfers between devices  24.8 us (43%)
  starting transfers between devices  19.5 us (34%)
  Pallas kernels  12.2 us (21%)
  between operations  0.79 us (1%)
    ppermute x20, waiting for transfers between devices, swap(): return lax.ppermute(array, axis, [(0, 1), (1, 0)])  24.8 us
    ppermute x20, starting transfers between devices, swap(): return lax.ppermute(array, axis, [(0, 1), (1, 0)])  19.5 us
    pallas_call x1, Pallas kernels, per_device(): call(functools.partial(early_body, rounds), [((1, rounds), jnp.int32)] +...  3.11 us
    pallas_call x1, Pallas kernels, per_device(): call(functools.partial(main_body, rounds, domains, where), [wide] * 3 + s...  2.15 us
    pallas_call x1, Pallas kernels, per_device(): call(node_body, [((nodes, features), BF16)], [VMEM] * (5 + rounds), kept=...  1.59 us
    pallas_call x1, Pallas kernels, per_device(): call(edge_body, [((nodes, features), BF16), wide], [VMEM] * 5, kept=False)  1.37 us
    pallas_call x2, Pallas kernels, per_device(): call(functools.partial(grads_body, domains, where), [shape] * len(group)...  1.25 us
  transfers between devices with their start and end apart: 20, of which 11 were waited for; matrix products, arithmetic and copies ran while one was open for 0% of the time, Pallas kernels for 13%

profile of v1, /device:TPU:0, one launch (start us, length us, event | category | flops | bytes accessed | tf_op | source)
XLA Modules:
  0.0 57.3 jit_solution(966708224688568208)
XLA Ops:
  0.6 1.0 %shard_map.148 = (bf16[128,512]{1,0:T(8,128)(2,1)S(1)}, bf16[128,512]{1,0:T(8,128)(2,1)S(1)}, bf16[128,512]{1,0:T(8,128)(2,1)S(1)}, bf16[128,512]{1,0:T(8,128)(2,1)S(1)}) custom-call(s32[4]{0:T(128)} %send_blocks.1, bf16[256,512]{1,0:T(8,128)(2,1)} %bitcast.13), custom_call_target="tpu_custom_call" | custom-call | tf_op jit(solution)/shard_map/pallas_call | solution.py:320
  2.2 2.6 %collective-permute-start.1 = (bf16[128,512]{1,0:T(8,128)(2,1)S(1)}, bf16[128,512]{1,0:T(8,128)(2,1)S(1)}, u32[]{:S(2)}, u32[]{:S(2)}) collective-permute-start(bf16[128,512]{1,0:T(8,128)(2,1)S(1)} %get-tuple-element.55), channel_id=1, source_target_pairs={{0,2},{2,0},{1,3},{3,1},{4,6},{6,4},{5,7},{7,5},{8,10},{10,8},{9,1... | collective-permute-start | bytes 393224 | tf_op jit(solution)/shard_map/ppermute | solution.py:52
  4.8 1.6 %collective-permute-start.2 = (bf16[128,512]{1,0:T(8,128)(2,1)S(1)}, bf16[128,512]{1,0:T(8,128)(2,1)S(1)}, u32[]{:S(2)}, u32[]{:S(2)}) collective-permute-start(bf16[128,512]{1,0:T(8,128)(2,1)S(1)} %get-tuple-element.56), channel_id=1, source_target_pairs={{0,4},{4,0},{1,5},{5,1},{2,6},{6,2},{3,7},{7,3},{8,12},{12,8},{9,1... | collective-permute-start | bytes 393224 | tf_op jit(solution)/shard_map/ppermute | solution.py:52
  6.4 2.6 %collective-permute-start.3 = (bf16[128,512]{1,0:T(8,128)(2,1)S(1)}, bf16[128,512]{1,0:T(8,128)(2,1)S(1)}, u32[]{:S(2)}, u32[]{:S(2)}) collective-permute-start(bf16[128,512]{1,0:T(8,128)(2,1)S(1)} %get-tuple-element.57), channel_id=1, source_target_pairs={{0,8},{8,0},{1,9},{9,1},{2,10},{10,2},{3,11},{11,3},{4,12},{12,4},... | collective-permute-start | bytes 393224 | tf_op jit(solution)/shard_map/ppermute | solution.py:52
  9.0 3.1 %shard_map.147 = (s32[1,4]{1,0:T(1,128)S(1)}, s32[1,512]{1,0:T(1,128)S(1)}, s32[1,512]{1,0:T(1,128)S(1)}, bf16[512,512]{1,0:T(8,128)(2,1)S(1)}, bf16[512,512]{1,...) custom-call(s32[4]{0:T(128)} %recv_block.1, ...), custom_call_target="tpu_custom_call" | custom-call | tf_op jit(solution)/shard_map/pallas_call | solution.py:324
  12.7 2.7 %collective-permute-done.3.refs_3_ = bf16[128,512]{1,0:T(8,128)(2,1)S(1)} collective-permute-done((bf16[128,512]{1,0:T(8,128)(2,1)S(1)}, bf16[128,512]{1,0:T(8,128)(2,1)S(1)}, u32[]{:S(2)}, u32[]{:S(2)}) %collective-permute-start.3) | collective-permute-done | bytes 131104 | tf_op jit(solution)/shard_map/ppermute | solution.py:52
  15.4 2.2 %shard_map.149 = (bf16[512,512]{1,0:T(8,128)(2,1)S(1)}, bf16[512,512]{1,0:T(8,128)(2,1)S(1)}, bf16[512,512]{1,0:T(8,128)(2,1)S(1)}, f32[16,32,512]{2,1,0:T(8,128)S(1)}, bf16[256,512]{1,0:T(8,128)(2,1)S(1)}) custom-call(bf16[512,512]{1,0:T(8,128)(2,1)S(1)} %get-tuple-element.50.send_own, bf16[512,512]{1,0:T(8,128)(2,1)S(1)} %get-tuple-element.51.hot, ...), custom_call_target="tpu_custom_call" | custom-call | tf_op jit(solution)/shard_map/pallas_call | solution.py:337
  17.6 0.8 %shard_map.153 = (f32[16,32,512]{2,1,0:T(8,128)S(1)}, f32[16,32,512]{2,1,0:T(8,128)S(1)}, bf16[512,512]{1,0:T(8,128)(2,1)S(1)}) custom-call(bf16[512,512]{1,0:T(8,128)(2,1)S(1)} %get-tuple-element.70.refs_0_, bf16[512,512]{1,0:T(8,128)(2,1)S(1)} %get-tuple-element.58.grad_preact.refs_1_.refs_3_, bf16[512,512]{1,0:T(8,128)(2,1)S(1)} %get-tuple-element.71.refs_2_, ...), custom_call_target="tpu_custom_call" | custom-call | tf_op jit(solution)/shard_map/pallas_call | solution.py:350
  19.5 1.1 %collective-permute-done.12.refs_2_ = bf16[256,512]{1,0:T(8,128)(2,1)S(1)} collective-permute-done((bf16[256,512]{1,0:T(8,128)(2,1)S(1)}, bf16[256,512]{1,0:T(8,128)(2,1)S(1)}, u32[]{:S(2)}, u32[]{:S(2)}) %collective-permute-start.12) | collective-permute-done | bytes 262176 | tf_op jit(solution)/shard_map/ppermute | solution.py:52
  21.1 1.6 %collective-permute-start.14 = (bf16[256,512]{1,0:T(8,128)(2,1)S(1)}, bf16[256,512]{1,0:T(8,128)(2,1)S(1)}, u32[]{:S(2)}, u32[]{:S(2)}) collective-permute-start(bf16[256,512]{1,0:T(8,128)(2,1)S(1)} %get-tuple-element.87), channel_id=1, source_target_pairs={{0,16},{16,0},{1,17},{17,1},{2,18},{18,2},{3,19},{19,3},{4,20},{20... | collective-permute-start | bytes 786440 | tf_op jit(solution)/shard_map/ppermute | solution.py:52
  23.4 6.2 %collective-permute-done.14.got = bf16[256,512]{1,0:T(8,128)(2,1)S(1)} collective-permute-done((bf16[256,512]{1,0:T(8,128)(2,1)S(1)}, bf16[256,512]{1,0:T(8,128)(2,1)S(1)}, u32[]{:S(2)}, u32[]{:S(2)}) %collective-permute-start.14) | collective-permute-done | bytes 262176 | tf_op jit(solution)/shard_map/ppermute | solution.py:52
  30.2 0.8 %collective-permute-done.9.got = bf16[256,512]{1,0:T(8,128)(2,1)S(1)} collective-permute-done((bf16[256,512]{1,0:T(8,128)(2,1)S(1)}, bf16[256,512]{1,0:T(8,128)(2,1)S(1)}, u32[]{:S(2)}, u32[]{:S(2)}) %collective-permute-start.9) | collective-permute-done | bytes 262176 | tf_op jit(solution)/shard_map/ppermute | solution.py:52
  31.5 3.1 %collective-permute-done.15.got = bf16[128,512]{1,0:T(8,128)(2,1)S(1)} collective-permute-done((bf16[128,512]{1,0:T(8,128)(2,1)S(1)}, bf16[128,512]{1,0:T(8,128)(2,1)S(1)}, u32[]{:S(2)}, u32[]{:S(2)}) %collective-permute-start.15) | collective-permute-done | bytes 131104 | tf_op jit(solution)/shard_map/ppermute | solution.py:52
  35.2 0.7 %shard_map.151 = (f32[256,512]{1,0:T(8,128)S(1)}, f32[256,512]{1,0:T(8,128)S(1)}, bf16[128,512]{1,0:T(8,128)(2,1)S(1)}, bf16[128,512]{1,0:T(8,128)(2,1)S(1)}, bf...) custom-call(s32[1,512]{1,0:T(1,128)S(1)} %get-tuple-element.63.edge_src, ...), custom_call_target="tpu_custom_call" | custom-call | tf_op jit(solution)/shard_map/pallas_call | solution.py:374
  35.9 0.7 %collective-permute-done.10.got = bf16[128,512]{1,0:T(8,128)(2,1)S(1)} collective-permute-done((bf16[128,512]{1,0:T(8,128)(2,1)S(1)}, bf16[128,512]{1,0:T(8,128)(2,1)S(1)}, u32[]{:S(2)}, u32[]{:S(2)}) %collective-permute-start.10) | collective-permute-done | bytes 131104 | tf_op jit(solution)/shard_map/ppermute | solution.py:52
  36.6 2.0 %collective-permute-start.11 = (bf16[64,512]{1,0:T(8,128)(2,1)S(1)}, bf16[64,512]{1,0:T(8,128)(2,1)S(1)}, u32[]{:S(2)}, u32[]{:S(2)}) collective-permute-start(bf16[64,512]{1,0:T(8,128)(2,1)S(1)} %get-tuple-element.80), channel_id=1, source_target_pairs={{0,8},{8,0},{1,9},{9,1},{2,10},{10,2},{3,11},{11,3},{4,12},{12,4},... | collective-permute-start | bytes 196616 | tf_op jit(solution)/shard_map/ppermute | solution.py:52
  39.1 1.5 %collective-permute-start.6 = (bf16[128,512]{1,0:T(8,128)(2,1)S(1)}, bf16[128,512]{1,0:T(8,128)(2,1)S(1)}, u32[]{:S(2)}, u32[]{:S(2)}) collective-permute-start(bf16[128,512]{1,0:T(8,128)(2,1)S(1)} %get-tuple-element.68), channel_id=1, source_target_pairs={{0,4},{4,0},{1,5},{5,1},{2,6},{6,2},{3,7},{7,3},{8,12},{12,8},{9,1... | collective-permute-start | bytes 393224 | tf_op jit(solution)/shard_map/ppermute | solution.py:52
  41.0 1.6 %collective-permute-done.11.got = bf16[64,512]{1,0:T(8,128)(2,1)S(1)} collective-permute-done((bf16[64,512]{1,0:T(8,128)(2,1)S(1)}, bf16[64,512]{1,0:T(8,128)(2,1)S(1)}, u32[]{:S(2)}, u32[]{:S(2)}) %collective-permute-start.11) | collective-permute-done | bytes 65568 | tf_op jit(solution)/shard_map/ppermute | solution.py:52
  42.6 1.2 %collective-permute-start.17 = (bf16[32,512]{1,0:T(8,128)(2,1)S(1)}, bf16[32,512]{1,0:T(8,128)(2,1)S(1)}, u32[]{:S(2)}, u32[]{:S(2)}) collective-permute-start(bf16[32,512]{1,0:T(8,128)(2,1)S(1)} %get-tuple-element.93), channel_id=1, source_target_pairs={{0,8},{8,0},{1,9},{9,1},{2,10},{10,2},{3,11},{11,3},{4,12},{12,4},... | collective-permute-start | bytes 98312 | tf_op jit(solution)/shard_map/ppermute | solution.py:52
  43.9 7.2 %collective-permute-done.17.got = bf16[32,512]{1,0:T(8,128)(2,1)S(1)} collective-permute-done((bf16[32,512]{1,0:T(8,128)(2,1)S(1)}, bf16[32,512]{1,0:T(8,128)(2,1)S(1)}, u32[]{:S(2)}, u32[]{:S(2)}) %collective-permute-start.17) | collective-permute-done | bytes 32800 | tf_op jit(solution)/shard_map/ppermute | solution.py:52
  51.1 1.5 %collective-permute-start.18 = (bf16[64,512]{1,0:T(8,128)(2,1)S(1)}, bf16[64,512]{1,0:T(8,128)(2,1)S(1)}, u32[]{:S(2)}, u32[]{:S(2)}) collective-permute-start(bf16[64,512]{1,0:T(8,128)(2,1)S(1)} %shard_map.157.refs_0_), channel_id=1, source_target_pairs={{0,16},{16,0},{1,17},{17,1},{2,18},{18,2},{3,19},{19,3},{4,20},{20... | collective-permute-start | bytes 196616 | tf_op jit(solution)/shard_map/ppermute | solution.py:52
  53.2 1.4 %shard_map.150 = (bf16[256,512]{1,0:T(8,128)(2,1)}, bf16[512,512]{1,0:T(8,128)(2,1)}) custom-call(s32[1,512]{1,0:T(1,128)S(1)} %get-tuple-element.49.receiver, bf16[512,512]{1,0:T(8,128)(2,1)S(1)} %get-tuple-element.58.grad_preact.refs_1_.refs_3_, bf16[512,512]{1,0:T(8,128)(2,1)S(1)} %get-tuple-element.59.message, bf16[512,512]{1,0:T(8,128)(2,1)S(1)} %bitcast.12, ...), custom_call_target="tpu_custom_call" | custom-call | tf_op jit(solution)/shard_map/pallas_call | solution.py:411
  54.6 1.6 %shard_map.152 = bf16[256,512]{1,0:T(8,128)(2,1)} custom-call(s32[1,4]{1,0:T(1,128)S(1)} %get-tuple-element.62.send_blocks, f32[256,512]{1,0:T(8,128)S(1)} %get-tuple-element.64.own_sums, f32[256,512]{1,0:T(8,128)S(1)} %get-tuple-element.65.recv_sums, bf16[512,512]{1,0:T(8,128)(2,1)S(1)} %copy-done.3, bf16[512,512]{1,0:T(8,128)(2,1)S(1)} %copy-done.2, ...), custom_call_target="tpu_custom_call" | custom-call | tf_op jit(solution)/shard_map/pallas_call | solution.py:414
  56.6 0.7 %shard_map.164 = f32[128,512]{1,0:T(8,128)} custom-call(bf16[64,512]{1,0:T(8,128)(2,1)S(1)} %shard_map.157.refs_0_, bf16[32,512]{1,0:T(8,128)(2,1)S(1)} %shard_map.163.refs_1_, bf16[64,512]{1,0:T(8,128)(2,1)S(1)} %collective-permute-done.18.refs_2_, bf16[32,512]{1,0:T(8,128)(2,1)S(1)} %collective-permute-done.19.refs_3_), custom_call_target="tpu_custom_call" | custom-call | tf_op jit(solution)/shard_map/pallas_call | solution.py:405
  (44 shorter events, 7.2 us)
Async XLA Ops:
  1.6 10.4 %collective-permute-start = (bf16[128,512]{1,0:T(8,128)(2,1)S(1)}, bf16[128,512]{1,0:T(8,128)(2,1)S(1)}, u32[]{:S(2)}, u32[]{:S(2)}) collective-permute-start(bf16[128,512]{1,0:T(8,128)(2,1)S(1)} %get-tuple-element.54), channel_id=1, source_target_pairs={{0,1},{1,0},{2,3},{3,2},{4,5},{5,4},{6,7},{7,6},{8,9},{9,8},{10,11... | collective-permute-start | bytes 393224 | tf_op jit(solution)/shard_map/ppermute | solution.py:52
  2.2 9.9 %collective-permute-start.1 = (bf16[128,512]{1,0:T(8,128)(2,1)S(1)}, bf16[128,512]{1,0:T(8,128)(2,1)S(1)}, u32[]{:S(2)}, u32[]{:S(2)}) collective-permute-start(bf16[128,512]{1,0:T(8,128)(2,1)S(1)} %get-tuple-element.55), channel_id=1, source_target_pairs={{0,2},{2,0},{1,3},{3,1},{4,6},{6,4},{5,7},{7,5},{8,10},{10,8},{9,1... | collective-permute-start | bytes 393224 | tf_op jit(solution)/shard_map/ppermute | solution.py:52
  4.8 7.9 %collective-permute-start.2 = (bf16[128,512]{1,0:T(8,128)(2,1)S(1)}, bf16[128,512]{1,0:T(8,128)(2,1)S(1)}, u32[]{:S(2)}, u32[]{:S(2)}) collective-permute-start(bf16[128,512]{1,0:T(8,128)(2,1)S(1)} %get-tuple-element.56), channel_id=1, source_target_pairs={{0,4},{4,0},{1,5},{5,1},{2,6},{6,2},{3,7},{7,3},{8,12},{12,8},{9,1... | collective-permute-start | bytes 393224 | tf_op jit(solution)/shard_map/ppermute | solution.py:52
  6.4 9.0 %collective-permute-start.3 = (bf16[128,512]{1,0:T(8,128)(2,1)S(1)}, bf16[128,512]{1,0:T(8,128)(2,1)S(1)}, u32[]{:S(2)}, u32[]{:S(2)}) collective-permute-start(bf16[128,512]{1,0:T(8,128)(2,1)S(1)} %get-tuple-element.57), channel_id=1, source_target_pairs={{0,8},{8,0},{1,9},{9,1},{2,10},{10,2},{3,11},{11,3},{4,12},{12,4},... | collective-permute-start | bytes 393224 | tf_op jit(solution)/shard_map/ppermute | solution.py:52
  8.9 6.4 %copy-start.3 = (bf16[512,512]{1,0:T(8,128)(2,1)S(1)}, bf16[512,512]{1,0:T(8,128)(2,1)}, u32[]{:S(2)}) copy-start(bf16[512,512]{1,0:T(8,128)(2,1)} %weight_send.3) | copy-start | bytes 1572868
  8.9 6.4 %copy-start.4 = (bf16[512,512]{1,0:T(8,128)(2,1)S(1)}, bf16[512,512]{1,0:T(8,128)(2,1)}, u32[]{:S(2)}) copy-start(bf16[512,512]{1,0:T(8,128)(2,1)} %weight_out.1) | copy-start | bytes 1572868
  18.3 4.4 %collective-permute-start.8 = (bf16[512,512]{1,0:T(8,128)(2,1)S(1)}, bf16[512,512]{1,0:T(8,128)(2,1)S(1)}, u32[]{:S(2)}, u32[]{:S(2)}) collective-permute-start(bf16[512,512]{1,0:T(8,128)(2,1)S(1)} %get-tuple-element.74), channel_id=1, source_target_pairs={{0,1},{1,0},{2,3},{3,2},{4,5},{5,4},{6,7},{7,6},{8,9},{9,8},{10,11... | collective-permute-start | bytes 1572872 | tf_op jit(solution)/shard_map/ppermute | solution.py:52
  18.4 2.3 %collective-permute-start.12 = (bf16[256,512]{1,0:T(8,128)(2,1)S(1)}, bf16[256,512]{1,0:T(8,128)(2,1)S(1)}, u32[]{:S(2)}, u32[]{:S(2)}) collective-permute-start(bf16[256,512]{1,0:T(8,128)(2,1)S(1)} %get-tuple-element.84), channel_id=1, source_target_pairs={{0,1},{1,0},{2,3},{3,2},{4,5},{5,4},{6,7},{7,6},{8,9},{9,8},{10,11... | collective-permute-start | bytes 786440 | tf_op jit(solution)/shard_map/ppermute | solution.py:52
  19.4 1.7 %collective-permute-start.13 = (bf16[256,512]{1,0:T(8,128)(2,1)S(1)}, bf16[256,512]{1,0:T(8,128)(2,1)S(1)}, u32[]{:S(2)}, u32[]{:S(2)}) collective-permute-start(bf16[256,512]{1,0:T(8,128)(2,1)S(1)} %get-tuple-element.85), channel_id=1, source_target_pairs={{0,1},{1,0},{2,3},{3,2},{4,5},{5,4},{6,7},{7,6},{8,9},{9,8},{10,11... | collective-permute-start | bytes 786440 | tf_op jit(solution)/shard_map/ppermute | solution.py:52
  21.1 8.4 %collective-permute-start.14 = (bf16[256,512]{1,0:T(8,128)(2,1)S(1)}, bf16[256,512]{1,0:T(8,128)(2,1)S(1)}, u32[]{:S(2)}, u32[]{:S(2)}) collective-permute-start(bf16[256,512]{1,0:T(8,128)(2,1)S(1)} %get-tuple-element.87), channel_id=1, source_target_pairs={{0,16},{16,0},{1,17},{17,1},{2,18},{18,2},{3,19},{19,3},{4,20},{20... | collective-permute-start | bytes 786440 | tf_op jit(solution)/shard_map/ppermute | solution.py:52
  22.8 8.1 %collective-permute-start.9 = (bf16[256,512]{1,0:T(8,128)(2,1)S(1)}, bf16[256,512]{1,0:T(8,128)(2,1)S(1)}, u32[]{:S(2)}, u32[]{:S(2)}) collective-permute-start(bf16[256,512]{1,0:T(8,128)(2,1)S(1)} %get-tuple-element.76), channel_id=1, source_target_pairs={{0,2},{2,0},{1,3},{3,1},{4,6},{6,4},{5,7},{7,5},{8,10},{10,8},{9,1... | collective-permute-start | bytes 786440 | tf_op jit(solution)/shard_map/ppermute | solution.py:52
  29.6 5.0 %collective-permute-start.15 = (bf16[128,512]{1,0:T(8,128)(2,1)S(1)}, bf16[128,512]{1,0:T(8,128)(2,1)S(1)}, u32[]{:S(2)}, u32[]{:S(2)}) collective-permute-start(bf16[128,512]{1,0:T(8,128)(2,1)S(1)} %get-tuple-element.89), channel_id=1, source_target_pairs={{0,2},{2,0},{1,3},{3,1},{4,6},{6,4},{5,7},{7,5},{8,10},{10,8},{9,1... | collective-permute-start | bytes 393224 | tf_op jit(solution)/shard_map/ppermute | solution.py:52
  31.0 5.6 %collective-permute-start.10 = (bf16[128,512]{1,0:T(8,128)(2,1)S(1)}, bf16[128,512]{1,0:T(8,128)(2,1)S(1)}, u32[]{:S(2)}, u32[]{:S(2)}) collective-permute-start(bf16[128,512]{1,0:T(8,128)(2,1)S(1)} %get-tuple-element.78), channel_id=1, source_target_pairs={{0,4},{4,0},{1,5},{5,1},{2,6},{6,2},{3,7},{7,3},{8,12},{12,8},{9,1... | collective-permute-start | bytes 393224 | tf_op jit(solution)/shard_map/ppermute | solution.py:52
  34.7 5.9 %collective-permute-start.16 = (bf16[64,512]{1,0:T(8,128)(2,1)S(1)}, bf16[64,512]{1,0:T(8,128)(2,1)S(1)}, u32[]{:S(2)}, u32[]{:S(2)}) collective-permute-start(bf16[64,512]{1,0:T(8,128)(2,1)S(1)} %get-tuple-element.91), channel_id=1, source_target_pairs={{0,4},{4,0},{1,5},{5,1},{2,6},{6,2},{3,7},{7,3},{8,12},{12,8},{9,1... | collective-permute-start | bytes 196616 | tf_op jit(solution)/shard_map/ppermute | solution.py:52
  35.2 18.0 %copy-start.1 = (bf16[512,512]{1,0:T(8,128)(2,1)S(1)}, bf16[512,512]{1,0:T(8,128)(2,1)}, u32[]{:S(2)}) copy-start(bf16[512,512]{1,0:T(8,128)(2,1)} %weight_edge.3) | copy-start | bytes 1572868
  35.9 17.3 %copy-start = (bf16[1,512,512]{2,1,0:T(8,128)(2,1)S(1)}, bf16[1,512,512]{2,1,0:T(8,128)(2,1)}, u32[]{:S(2)}) copy-start(bf16[1,512,512]{2,1,0:T(8,128)(2,1)} %param.14) | copy-start | bytes 1572868
  36.6 6.0 %collective-permute-start.11 = (bf16[64,512]{1,0:T(8,128)(2,1)S(1)}, bf16[64,512]{1,0:T(8,128)(2,1)S(1)}, u32[]{:S(2)}, u32[]{:S(2)}) collective-permute-start(bf16[64,512]{1,0:T(8,128)(2,1)S(1)} %get-tuple-element.80), channel_id=1, source_target_pairs={{0,8},{8,0},{1,9},{9,1},{2,10},{10,2},{3,11},{11,3},{4,12},{12,4},... | collective-permute-start | bytes 196616 | tf_op jit(solution)/shard_map/ppermute | solution.py:52
  38.6 14.0 %collective-permute-start.4 = (bf16[128,512]{1,0:T(8,128)(2,1)S(1)}, bf16[128,512]{1,0:T(8,128)(2,1)S(1)}, u32[]{:S(2)}, u32[]{:S(2)}) collective-permute-start(bf16[128,512]{1,0:T(8,128)(2,1)S(1)} %get-tuple-element.66), channel_id=1, source_target_pairs={{0,1},{1,0},{2,3},{3,2},{4,5},{5,4},{6,7},{7,6},{8,9},{9,8},{10,11... | collective-permute-start | bytes 393224 | tf_op jit(solution)/shard_map/ppermute | solution.py:52
  38.6 16.0 %collective-permute-start.5 = (bf16[128,512]{1,0:T(8,128)(2,1)S(1)}, bf16[128,512]{1,0:T(8,128)(2,1)S(1)}, u32[]{:S(2)}, u32[]{:S(2)}) collective-permute-start(bf16[128,512]{1,0:T(8,128)(2,1)S(1)} %get-tuple-element.67), channel_id=1, source_target_pairs={{0,2},{2,0},{1,3},{3,1},{4,6},{6,4},{5,7},{7,5},{8,10},{10,8},{9,1... | collective-permute-start | bytes 393224 | tf_op jit(solution)/shard_map/ppermute | solution.py:52
  39.1 15.5 %collective-permute-start.6 = (bf16[128,512]{1,0:T(8,128)(2,1)S(1)}, bf16[128,512]{1,0:T(8,128)(2,1)S(1)}, u32[]{:S(2)}, u32[]{:S(2)}) collective-permute-start(bf16[128,512]{1,0:T(8,128)(2,1)S(1)} %get-tuple-element.68), channel_id=1, source_target_pairs={{0,4},{4,0},{1,5},{5,1},{2,6},{6,2},{3,7},{7,3},{8,12},{12,8},{9,1... | collective-permute-start | bytes 393224 | tf_op jit(solution)/shard_map/ppermute | solution.py:52
  40.6 14.0 %collective-permute-start.7 = (bf16[128,512]{1,0:T(8,128)(2,1)S(1)}, bf16[128,512]{1,0:T(8,128)(2,1)S(1)}, u32[]{:S(2)}, u32[]{:S(2)}) collective-permute-start(bf16[128,512]{1,0:T(8,128)(2,1)S(1)} %get-tuple-element.69), channel_id=1, source_target_pairs={{0,8},{8,0},{1,9},{9,1},{2,10},{10,2},{3,11},{11,3},{4,12},{12,4},... | collective-permute-start | bytes 393224 | tf_op jit(solution)/shard_map/ppermute | solution.py:52
  42.6 8.4 %collective-permute-start.17 = (bf16[32,512]{1,0:T(8,128)(2,1)S(1)}, bf16[32,512]{1,0:T(8,128)(2,1)S(1)}, u32[]{:S(2)}, u32[]{:S(2)}) collective-permute-start(bf16[32,512]{1,0:T(8,128)(2,1)S(1)} %get-tuple-element.93), channel_id=1, source_target_pairs={{0,8},{8,0},{1,9},{9,1},{2,10},{10,2},{3,11},{11,3},{4,12},{12,4},... | collective-permute-start | bytes 98312 | tf_op jit(solution)/shard_map/ppermute | solution.py:52
  51.1 5.5 %collective-permute-start.18 = (bf16[64,512]{1,0:T(8,128)(2,1)S(1)}, bf16[64,512]{1,0:T(8,128)(2,1)S(1)}, u32[]{:S(2)}, u32[]{:S(2)}) collective-permute-start(bf16[64,512]{1,0:T(8,128)(2,1)S(1)} %shard_map.157.refs_0_), channel_id=1, source_target_pairs={{0,16},{16,0},{1,17},{17,1},{2,18},{18,2},{3,19},{19,3},{4,20},{20... | collective-permute-start | bytes 196616 | tf_op jit(solution)/shard_map/ppermute | solution.py:52
  52.6 4.0 %collective-permute-start.19 = (bf16[32,512]{1,0:T(8,128)(2,1)S(1)}, bf16[32,512]{1,0:T(8,128)(2,1)S(1)}, u32[]{:S(2)}, u32[]{:S(2)}) collective-permute-start(bf16[32,512]{1,0:T(8,128)(2,1)S(1)} %shard_map.163.refs_1_), channel_id=1, source_target_pairs={{0,16},{16,0},{1,17},{17,1},{2,18},{18,2},{3,19},{19,3},{4,20},{20... | collective-permute-start | bytes 98312 | tf_op jit(solution)/shard_map/ppermute | solution.py:52
  (1 other events, 1.4 us)

commit v2 on v1

--- a/solution.py
+++ b/solution.py
@@ -145,8 +145,9 @@
     send_out[...] = send
     preact = preact_own[...] + dot(send, weight_send[...])
     sigmoid = jax.nn.sigmoid(preact)
-    hidden = (preact * sigmoid).astype(BF16)
-    slope = sigmoid * (1.0 + preact * (1.0 - sigmoid))
+    product = preact * sigmoid
+    hidden = product.astype(BF16)
+    slope = sigmoid + product * (1.0 - sigmoid)
     projected = dot(hidden, weight_out[...])
     centered = projected - jnp.mean(projected, axis=1, keepdims=True)
     inv_std = lax.rsqrt(jnp.mean(centered * centered, axis=1, keepdims=True) + 1e-05)

time: 57.4 us -> 57.4 us (level)
  no operation moved by 1% of the time
where the time goes in v2:
time: 57.4 us; the launch traced here: 57.3 us
  waiting for transfers between devices  24.8 us (43%)
  starting transfers between devices  19.5 us (34%)
  Pallas kernels  12.2 us (21%)
  between operations  0.79 us (1%)
    ppermute x20, waiting for transfers between devices, swap(): return lax.ppermute(array, axis, [(0, 1), (1, 0)])  24.8 us
    ppermute x20, starting transfers between devices, swap(): return lax.ppermute(array, axis, [(0, 1), (1, 0)])  19.5 us
    pallas_call x1, Pallas kernels, per_device(): call(functools.partial(early_body, rounds), [((1, rounds), jnp.int32)] +...  3.11 us
    pallas_call x1, Pallas kernels, per_device(): call(functools.partial(main_body, rounds, domains, where), [wide] * 3 + s...  2.12 us
    pallas_call x1, Pallas kernels, per_device(): call(node_body, [((nodes, features), BF16)], [VMEM] * (5 + rounds), kept=...  1.59 us
    pallas_call x1, Pallas kernels, per_device(): call(edge_body, [((nodes, features), BF16), wide], [VMEM] * 5, kept=False)  1.37 us
    pallas_call x2, Pallas kernels, per_device(): call(functools.partial(grads_body, domains, where), [shape] * len(group)...  1.25 us
  transfers between devices with their start and end apart: 20, of which 11 were waited for; matrix products, arithmetic and copies ran while one was open for 0% of the time, Pallas kernels for 13%

profile of v2, /device:TPU:0, one launch (start us, length us, event | category | flops | bytes accessed | tf_op | source)
XLA Modules:
  0.0 57.3 jit_solution(1418191172308811339)
XLA Ops:
  0.6 1.0 %shard_map.148 = (bf16[128,512]{1,0:T(8,128)(2,1)S(1)}, bf16[128,512]{1,0:T(8,128)(2,1)S(1)}, bf16[128,512]{1,0:T(8,128)(2,1)S(1)}, bf16[128,512]{1,0:T(8,128)(2,1)S(1)}) custom-call(s32[4]{0:T(128)} %send_blocks.1, bf16[256,512]{1,0:T(8,128)(2,1)} %bitcast.13), custom_call_target="tpu_custom_call" | custom-call | tf_op jit(solution)/shard_map/pallas_call | solution.py:321
  2.2 2.6 %collective-permute-start.1 = (bf16[128,512]{1,0:T(8,128)(2,1)S(1)}, bf16[128,512]{1,0:T(8,128)(2,1)S(1)}, u32[]{:S(2)}, u32[]{:S(2)}) collective-permute-start(bf16[128,512]{1,0:T(8,128)(2,1)S(1)} %get-tuple-element.55), channel_id=1, source_target_pairs={{0,2},{2,0},{1,3},{3,1},{4,6},{6,4},{5,7},{7,5},{8,10},{10,8},{9,1... | collective-permute-start | bytes 393224 | tf_op jit(solution)/shard_map/ppermute | solution.py:52
  4.8 1.6 %collective-permute-start.2 = (bf16[128,512]{1,0:T(8,128)(2,1)S(1)}, bf16[128,512]{1,0:T(8,128)(2,1)S(1)}, u32[]{:S(2)}, u32[]{:S(2)}) collective-permute-start(bf16[128,512]{1,0:T(8,128)(2,1)S(1)} %get-tuple-element.56), channel_id=1, source_target_pairs={{0,4},{4,0},{1,5},{5,1},{2,6},{6,2},{3,7},{7,3},{8,12},{12,8},{9,1... | collective-permute-start | bytes 393224 | tf_op jit(solution)/shard_map/ppermute | solution.py:52
  6.4 2.6 %collective-permute-start.3 = (bf16[128,512]{1,0:T(8,128)(2,1)S(1)}, bf16[128,512]{1,0:T(8,128)(2,1)S(1)}, u32[]{:S(2)}, u32[]{:S(2)}) collective-permute-start(bf16[128,512]{1,0:T(8,128)(2,1)S(1)} %get-tuple-element.57), channel_id=1, source_target_pairs={{0,8},{8,0},{1,9},{9,1},{2,10},{10,2},{3,11},{11,3},{4,12},{12,4},... | collective-permute-start | bytes 393224 | tf_op jit(solution)/shard_map/ppermute | solution.py:52
  9.0 3.1 %shard_map.147 = (s32[1,4]{1,0:T(1,128)S(1)}, s32[1,512]{1,0:T(1,128)S(1)}, s32[1,512]{1,0:T(1,128)S(1)}, bf16[512,512]{1,0:T(8,128)(2,1)S(1)}, bf16[512,512]{1,...) custom-call(s32[4]{0:T(128)} %recv_block.1, ...), custom_call_target="tpu_custom_call" | custom-call | tf_op jit(solution)/shard_map/pallas_call | solution.py:325
  12.7 2.7 %collective-permute-done.3.refs_3_ = bf16[128,512]{1,0:T(8,128)(2,1)S(1)} collective-permute-done((bf16[128,512]{1,0:T(8,128)(2,1)S(1)}, bf16[128,512]{1,0:T(8,128)(2,1)S(1)}, u32[]{:S(2)}, u32[]{:S(2)}) %collective-permute-start.3) | collective-permute-done | bytes 131104 | tf_op jit(solution)/shard_map/ppermute | solution.py:52
  15.4 2.1 %shard_map.149 = (bf16[512,512]{1,0:T(8,128)(2,1)S(1)}, bf16[512,512]{1,0:T(8,128)(2,1)S(1)}, bf16[512,512]{1,0:T(8,128)(2,1)S(1)}, f32[16,32,512]{2,1,0:T(8,128)S(1)}, bf16[256,512]{1,0:T(8,128)(2,1)S(1)}) custom-call(bf16[512,512]{1,0:T(8,128)(2,1)S(1)} %get-tuple-element.50.send_own, bf16[512,512]{1,0:T(8,128)(2,1)S(1)} %get-tuple-element.51.hot, ...), custom_call_target="tpu_custom_call" | custom-call | tf_op jit(solution)/shard_map/pallas_call | solution.py:338
  17.5 0.8 %shard_map.153 = (f32[16,32,512]{2,1,0:T(8,128)S(1)}, f32[16,32,512]{2,1,0:T(8,128)S(1)}, bf16[512,512]{1,0:T(8,128)(2,1)S(1)}) custom-call(bf16[512,512]{1,0:T(8,128)(2,1)S(1)} %get-tuple-element.70.refs_0_, bf16[512,512]{1,0:T(8,128)(2,1)S(1)} %get-tuple-element.58.grad_preact.refs_1_.refs_3_, bf16[512,512]{1,0:T(8,128)(2,1)S(1)} %get-tuple-element.71.refs_2_, ...), custom_call_target="tpu_custom_call" | custom-call | tf_op jit(solution)/shard_map/pallas_call | solution.py:351
  19.5 1.1 %collective-permute-done.12.refs_2_ = bf16[256,512]{1,0:T(8,128)(2,1)S(1)} collective-permute-done((bf16[256,512]{1,0:T(8,128)(2,1)S(1)}, bf16[256,512]{1,0:T(8,128)(2,1)S(1)}, u32[]{:S(2)}, u32[]{:S(2)}) %collective-permute-start.12) | collective-permute-done | bytes 262176 | tf_op jit(solution)/shard_map/ppermute | solution.py:52
  21.1 1.6 %collective-permute-start.14 = (bf16[256,512]{1,0:T(8,128)(2,1)S(1)}, bf16[256,512]{1,0:T(8,128)(2,1)S(1)}, u32[]{:S(2)}, u32[]{:S(2)}) collective-permute-start(bf16[256,512]{1,0:T(8,128)(2,1)S(1)} %get-tuple-element.87), channel_id=1, source_target_pairs={{0,16},{16,0},{1,17},{17,1},{2,18},{18,2},{3,19},{19,3},{4,20},{20... | collective-permute-start | bytes 786440 | tf_op jit(solution)/shard_map/ppermute | solution.py:52
  23.3 6.2 %collective-permute-done.14.got = bf16[256,512]{1,0:T(8,128)(2,1)S(1)} collective-permute-done((bf16[256,512]{1,0:T(8,128)(2,1)S(1)}, bf16[256,512]{1,0:T(8,128)(2,1)S(1)}, u32[]{:S(2)}, u32[]{:S(2)}) %collective-permute-start.14) | collective-permute-done | bytes 262176 | tf_op jit(solution)/shard_map/ppermute | solution.py:52
  30.1 0.8 %collective-permute-done.9.got = bf16[256,512]{1,0:T(8,128)(2,1)S(1)} collective-permute-done((bf16[256,512]{1,0:T(8,128)(2,1)S(1)}, bf16[256,512]{1,0:T(8,128)(2,1)S(1)}, u32[]{:S(2)}, u32[]{:S(2)}) %collective-permute-start.9) | collective-permute-done | bytes 262176 | tf_op jit(solution)/shard_map/ppermute | solution.py:52
  31.5 3.1 %collective-permute-done.15.got = bf16[128,512]{1,0:T(8,128)(2,1)S(1)} collective-permute-done((bf16[128,512]{1,0:T(8,128)(2,1)S(1)}, bf16[128,512]{1,0:T(8,128)(2,1)S(1)}, u32[]{:S(2)}, u32[]{:S(2)}) %collective-permute-start.15) | collective-permute-done | bytes 131104 | tf_op jit(solution)/shard_map/ppermute | solution.py:52
  35.1 0.7 %shard_map.151 = (f32[256,512]{1,0:T(8,128)S(1)}, f32[256,512]{1,0:T(8,128)S(1)}, bf16[128,512]{1,0:T(8,128)(2,1)S(1)}, bf16[128,512]{1,0:T(8,128)(2,1)S(1)}, bf...) custom-call(s32[1,512]{1,0:T(1,128)S(1)} %get-tuple-element.63.edge_src, ...), custom_call_target="tpu_custom_call" | custom-call | tf_op jit(solution)/shard_map/pallas_call | solution.py:375
  35.9 0.7 %collective-permute-done.10.got = bf16[128,512]{1,0:T(8,128)(2,1)S(1)} collective-permute-done((bf16[128,512]{1,0:T(8,128)(2,1)S(1)}, bf16[128,512]{1,0:T(8,128)(2,1)S(1)}, u32[]{:S(2)}, u32[]{:S(2)}) %collective-permute-start.10) | collective-permute-done | bytes 131104 | tf_op jit(solution)/shard_map/ppermute | solution.py:52
  36.6 2.0 %collective-permute-start.11 = (bf16[64,512]{1,0:T(8,128)(2,1)S(1)}, bf16[64,512]{1,0:T(8,128)(2,1)S(1)}, u32[]{:S(2)}, u32[]{:S(2)}) collective-permute-start(bf16[64,512]{1,0:T(8,128)(2,1)S(1)} %get-tuple-element.80), channel_id=1, source_target_pairs={{0,8},{8,0},{1,9},{9,1},{2,10},{10,2},{3,11},{11,3},{4,12},{12,4},... | collective-permute-start | bytes 196616 | tf_op jit(solution)/shard_map/ppermute | solution.py:52
  39.1 1.5 %collective-permute-start.6 = (bf16[128,512]{1,0:T(8,128)(2,1)S(1)}, bf16[128,512]{1,0:T(8,128)(2,1)S(1)}, u32[]{:S(2)}, u32[]{:S(2)}) collective-permute-start(bf16[128,512]{1,0:T(8,128)(2,1)S(1)} %get-tuple-element.68), channel_id=1, source_target_pairs={{0,4},{4,0},{1,5},{5,1},{2,6},{6,2},{3,7},{7,3},{8,12},{12,8},{9,1... | collective-permute-start | bytes 393224 | tf_op jit(solution)/shard_map/ppermute | solution.py:52
  41.0 1.6 %collective-permute-done.11.got = bf16[64,512]{1,0:T(8,128)(2,1)S(1)} collective-permute-done((bf16[64,512]{1,0:T(8,128)(2,1)S(1)}, bf16[64,512]{1,0:T(8,128)(2,1)S(1)}, u32[]{:S(2)}, u32[]{:S(2)}) %collective-permute-start.11) | collective-permute-done | bytes 65568 | tf_op jit(solution)/shard_map/ppermute | solution.py:52
  42.6 1.2 %collective-permute-start.17 = (bf16[32,512]{1,0:T(8,128)(2,1)S(1)}, bf16[32,512]{1,0:T(8,128)(2,1)S(1)}, u32[]{:S(2)}, u32[]{:S(2)}) collective-permute-start(bf16[32,512]{1,0:T(8,128)(2,1)S(1)} %get-tuple-element.93), channel_id=1, source_target_pairs={{0,8},{8,0},{1,9},{9,1},{2,10},{10,2},{3,11},{11,3},{4,12},{12,4},... | collective-permute-start | bytes 98312 | tf_op jit(solution)/shard_map/ppermute | solution.py:52
  43.8 7.2 %collective-permute-done.17.got = bf16[32,512]{1,0:T(8,128)(2,1)S(1)} collective-permute-done((bf16[32,512]{1,0:T(8,128)(2,1)S(1)}, bf16[32,512]{1,0:T(8,128)(2,1)S(1)}, u32[]{:S(2)}, u32[]{:S(2)}) %collective-permute-start.17) | collective-permute-done | bytes 32800 | tf_op jit(solution)/shard_map/ppermute | solution.py:52
  51.0 1.5 %collective-permute-start.18 = (bf16[64,512]{1,0:T(8,128)(2,1)S(1)}, bf16[64,512]{1,0:T(8,128)(2,1)S(1)}, u32[]{:S(2)}, u32[]{:S(2)}) collective-permute-start(bf16[64,512]{1,0:T(8,128)(2,1)S(1)} %shard_map.157.refs_0_), channel_id=1, source_target_pairs={{0,16},{16,0},{1,17},{17,1},{2,18},{18,2},{3,19},{19,3},{4,20},{20... | collective-permute-start | bytes 196616 | tf_op jit(solution)/shard_map/ppermute | solution.py:52
  53.2 1.4 %shard_map.150 = (bf16[256,512]{1,0:T(8,128)(2,1)}, bf16[512,512]{1,0:T(8,128)(2,1)}) custom-call(s32[1,512]{1,0:T(1,128)S(1)} %get-tuple-element.49.receiver, bf16[512,512]{1,0:T(8,128)(2,1)S(1)} %get-tuple-element.58.grad_preact.refs_1_.refs_3_, bf16[512,512]{1,0:T(8,128)(2,1)S(1)} %get-tuple-element.59.message, bf16[512,512]{1,0:T(8,128)(2,1)S(1)} %bitcast.12, ...), custom_call_target="tpu_custom_call" | custom-call | tf_op jit(solution)/shard_map/pallas_call | solution.py:412
  54.6 1.6 %shard_map.152 = bf16[256,512]{1,0:T(8,128)(2,1)} custom-call(s32[1,4]{1,0:T(1,128)S(1)} %get-tuple-element.62.send_blocks, f32[256,512]{1,0:T(8,128)S(1)} %get-tuple-element.64.own_sums, f32[256,512]{1,0:T(8,128)S(1)} %get-tuple-element.65.recv_sums, bf16[512,512]{1,0:T(8,128)(2,1)S(1)} %copy-done.3, bf16[512,512]{1,0:T(8,128)(2,1)S(1)} %copy-done.2, ...), custom_call_target="tpu_custom_call" | custom-call | tf_op jit(solution)/shard_map/pallas_call | solution.py:415
  56.5 0.7 %shard_map.164 = f32[128,512]{1,0:T(8,128)} custom-call(bf16[64,512]{1,0:T(8,128)(2,1)S(1)} %shard_map.157.refs_0_, bf16[32,512]{1,0:T(8,128)(2,1)S(1)} %shard_map.163.refs_1_, bf16[64,512]{1,0:T(8,128)(2,1)S(1)} %collective-permute-done.18.refs_2_, bf16[32,512]{1,0:T(8,128)(2,1)S(1)} %collective-permute-done.19.refs_3_), custom_call_target="tpu_custom_call" | custom-call | tf_op jit(solution)/shard_map/pallas_call | solution.py:406
  (44 shorter events, 7.2 us)
Async XLA Ops:
  1.6 10.4 %collective-permute-start = (bf16[128,512]{1,0:T(8,128)(2,1)S(1)}, bf16[128,512]{1,0:T(8,128)(2,1)S(1)}, u32[]{:S(2)}, u32[]{:S(2)}) collective-permute-start(bf16[128,512]{1,0:T(8,128)(2,1)S(1)} %get-tuple-element.54), channel_id=1, source_target_pairs={{0,1},{1,0},{2,3},{3,2},{4,5},{5,4},{6,7},{7,6},{8,9},{9,8},{10,11... | collective-permute-start | bytes 393224 | tf_op jit(solution)/shard_map/ppermute | solution.py:52
  2.2 9.9 %collective-permute-start.1 = (bf16[128,512]{1,0:T(8,128)(2,1)S(1)}, bf16[128,512]{1,0:T(8,128)(2,1)S(1)}, u32[]{:S(2)}, u32[]{:S(2)}) collective-permute-start(bf16[128,512]{1,0:T(8,128)(2,1)S(1)} %get-tuple-element.55), channel_id=1, source_target_pairs={{0,2},{2,0},{1,3},{3,1},{4,6},{6,4},{5,7},{7,5},{8,10},{10,8},{9,1... | collective-permute-start | bytes 393224 | tf_op jit(solution)/shard_map/ppermute | solution.py:52
  4.8 7.9 %collective-permute-start.2 = (bf16[128,512]{1,0:T(8,128)(2,1)S(1)}, bf16[128,512]{1,0:T(8,128)(2,1)S(1)}, u32[]{:S(2)}, u32[]{:S(2)}) collective-permute-start(bf16[128,512]{1,0:T(8,128)(2,1)S(1)} %get-tuple-element.56), channel_id=1, source_target_pairs={{0,4},{4,0},{1,5},{5,1},{2,6},{6,2},{3,7},{7,3},{8,12},{12,8},{9,1... | collective-permute-start | bytes 393224 | tf_op jit(solution)/shard_map/ppermute | solution.py:52
  6.4 9.0 %collective-permute-start.3 = (bf16[128,512]{1,0:T(8,128)(2,1)S(1)}, bf16[128,512]{1,0:T(8,128)(2,1)S(1)}, u32[]{:S(2)}, u32[]{:S(2)}) collective-permute-start(bf16[128,512]{1,0:T(8,128)(2,1)S(1)} %get-tuple-element.57), channel_id=1, source_target_pairs={{0,8},{8,0},{1,9},{9,1},{2,10},{10,2},{3,11},{11,3},{4,12},{12,4},... | collective-permute-start | bytes 393224 | tf_op jit(solution)/shard_map/ppermute | solution.py:52
  8.9 6.4 %copy-start.3 = (bf16[512,512]{1,0:T(8,128)(2,1)S(1)}, bf16[512,512]{1,0:T(8,128)(2,1)}, u32[]{:S(2)}) copy-start(bf16[512,512]{1,0:T(8,128)(2,1)} %weight_send.3) | copy-start | bytes 1572868
  8.9 6.4 %copy-start.4 = (bf16[512,512]{1,0:T(8,128)(2,1)S(1)}, bf16[512,512]{1,0:T(8,128)(2,1)}, u32[]{:S(2)}) copy-start(bf16[512,512]{1,0:T(8,128)(2,1)} %weight_out.1) | copy-start | bytes 1572868
  18.3 4.4 %collective-permute-start.8 = (bf16[512,512]{1,0:T(8,128)(2,1)S(1)}, bf16[512,512]{1,0:T(8,128)(2,1)S(1)}, u32[]{:S(2)}, u32[]{:S(2)}) collective-permute-start(bf16[512,512]{1,0:T(8,128)(2,1)S(1)} %get-tuple-element.74), channel_id=1, source_target_pairs={{0,1},{1,0},{2,3},{3,2},{4,5},{5,4},{6,7},{7,6},{8,9},{9,8},{10,11... | collective-permute-start | bytes 1572872 | tf_op jit(solution)/shard_map/ppermute | solution.py:52
  18.4 2.3 %collective-permute-start.12 = (bf16[256,512]{1,0:T(8,128)(2,1)S(1)}, bf16[256,512]{1,0:T(8,128)(2,1)S(1)}, u32[]{:S(2)}, u32[]{:S(2)}) collective-permute-start(bf16[256,512]{1,0:T(8,128)(2,1)S(1)} %get-tuple-element.84), channel_id=1, source_target_pairs={{0,1},{1,0},{2,3},{3,2},{4,5},{5,4},{6,7},{7,6},{8,9},{9,8},{10,11... | collective-permute-start | bytes 786440 | tf_op jit(solution)/shard_map/ppermute | solution.py:52
  19.4 1.7 %collective-permute-start.13 = (bf16[256,512]{1,0:T(8,128)(2,1)S(1)}, bf16[256,512]{1,0:T(8,128)(2,1)S(1)}, u32[]{:S(2)}, u32[]{:S(2)}) collective-permute-start(bf16[256,512]{1,0:T(8,128)(2,1)S(1)} %get-tuple-element.85), channel_id=1, source_target_pairs={{0,1},{1,0},{2,3},{3,2},{4,5},{5,4},{6,7},{7,6},{8,9},{9,8},{10,11... | collective-permute-start | bytes 786440 | tf_op jit(solution)/shard_map/ppermute | solution.py:52
  21.1 8.4 %collective-permute-start.14 = (bf16[256,512]{1,0:T(8,128)(2,1)S(1)}, bf16[256,512]{1,0:T(8,128)(2,1)S(1)}, u32[]{:S(2)}, u32[]{:S(2)}) collective-permute-start(bf16[256,512]{1,0:T(8,128)(2,1)S(1)} %get-tuple-element.87), channel_id=1, source_target_pairs={{0,16},{16,0},{1,17},{17,1},{2,18},{18,2},{3,19},{19,3},{4,20},{20... | collective-permute-start | bytes 786440 | tf_op jit(solution)/shard_map/ppermute | solution.py:52
  22.8 8.1 %collective-permute-start.9 = (bf16[256,512]{1,0:T(8,128)(2,1)S(1)}, bf16[256,512]{1,0:T(8,128)(2,1)S(1)}, u32[]{:S(2)}, u32[]{:S(2)}) collective-permute-start(bf16[256,512]{1,0:T(8,128)(2,1)S(1)} %get-tuple-element.76), channel_id=1, source_target_pairs={{0,2},{2,0},{1,3},{3,1},{4,6},{6,4},{5,7},{7,5},{8,10},{10,8},{9,1... | collective-permute-start | bytes 786440 | tf_op jit(solution)/shard_map/ppermute | solution.py:52
  29.6 5.0 %collective-permute-start.15 = (bf16[128,512]{1,0:T(8,128)(2,1)S(1)}, bf16[128,512]{1,0:T(8,128)(2,1)S(1)}, u32[]{:S(2)}, u32[]{:S(2)}) collective-permute-start(bf16[128,512]{1,0:T(8,128)(2,1)S(1)} %get-tuple-element.89), channel_id=1, source_target_pairs={{0,2},{2,0},{1,3},{3,1},{4,6},{6,4},{5,7},{7,5},{8,10},{10,8},{9,1... | collective-permute-start | bytes 393224 | tf_op jit(solution)/shard_map/ppermute | solution.py:52
  31.0 5.6 %collective-permute-start.10 = (bf16[128,512]{1,0:T(8,128)(2,1)S(1)}, bf16[128,512]{1,0:T(8,128)(2,1)S(1)}, u32[]{:S(2)}, u32[]{:S(2)}) collective-permute-start(bf16[128,512]{1,0:T(8,128)(2,1)S(1)} %get-tuple-element.78), channel_id=1, source_target_pairs={{0,4},{4,0},{1,5},{5,1},{2,6},{6,2},{3,7},{7,3},{8,12},{12,8},{9,1... | collective-permute-start | bytes 393224 | tf_op jit(solution)/shard_map/ppermute | solution.py:52
  34.6 6.0 %collective-permute-start.16 = (bf16[64,512]{1,0:T(8,128)(2,1)S(1)}, bf16[64,512]{1,0:T(8,128)(2,1)S(1)}, u32[]{:S(2)}, u32[]{:S(2)}) collective-permute-start(bf16[64,512]{1,0:T(8,128)(2,1)S(1)} %get-tuple-element.91), channel_id=1, source_target_pairs={{0,4},{4,0},{1,5},{5,1},{2,6},{6,2},{3,7},{7,3},{8,12},{12,8},{9,1... | collective-permute-start | bytes 196616 | tf_op jit(solution)/shard_map/ppermute | solution.py:52
  35.1 18.0 %copy-start.1 = (bf16[512,512]{1,0:T(8,128)(2,1)S(1)}, bf16[512,512]{1,0:T(8,128)(2,1)}, u32[]{:S(2)}) copy-start(bf16[512,512]{1,0:T(8,128)(2,1)} %weight_edge.3) | copy-start | bytes 1572868
  35.9 17.3 %copy-start = (bf16[1,512,512]{2,1,0:T(8,128)(2,1)S(1)}, bf16[1,512,512]{2,1,0:T(8,128)(2,1)}, u32[]{:S(2)}) copy-start(bf16[1,512,512]{2,1,0:T(8,128)(2,1)} %param.14) | copy-start | bytes 1572868
  36.6 6.0 %collective-permute-start.11 = (bf16[64,512]{1,0:T(8,128)(2,1)S(1)}, bf16[64,512]{1,0:T(8,128)(2,1)S(1)}, u32[]{:S(2)}, u32[]{:S(2)}) collective-permute-start(bf16[64,512]{1,0:T(8,128)(2,1)S(1)} %get-tuple-element.80), channel_id=1, source_target_pairs={{0,8},{8,0},{1,9},{9,1},{2,10},{10,2},{3,11},{11,3},{4,12},{12,4},... | collective-permute-start | bytes 196616 | tf_op jit(solution)/shard_map/ppermute | solution.py:52
  38.6 14.0 %collective-permute-start.4 = (bf16[128,512]{1,0:T(8,128)(2,1)S(1)}, bf16[128,512]{1,0:T(8,128)(2,1)S(1)}, u32[]{:S(2)}, u32[]{:S(2)}) collective-permute-start(bf16[128,512]{1,0:T(8,128)(2,1)S(1)} %get-tuple-element.66), channel_id=1, source_target_pairs={{0,1},{1,0},{2,3},{3,2},{4,5},{5,4},{6,7},{7,6},{8,9},{9,8},{10,11... | collective-permute-start | bytes 393224 | tf_op jit(solution)/shard_map/ppermute | solution.py:52
  38.6 16.0 %collective-permute-start.5 = (bf16[128,512]{1,0:T(8,128)(2,1)S(1)}, bf16[128,512]{1,0:T(8,128)(2,1)S(1)}, u32[]{:S(2)}, u32[]{:S(2)}) collective-permute-start(bf16[128,512]{1,0:T(8,128)(2,1)S(1)} %get-tuple-element.67), channel_id=1, source_target_pairs={{0,2},{2,0},{1,3},{3,1},{4,6},{6,4},{5,7},{7,5},{8,10},{10,8},{9,1... | collective-permute-start | bytes 393224 | tf_op jit(solution)/shard_map/ppermute | solution.py:52
  39.1 15.5 %collective-permute-start.6 = (bf16[128,512]{1,0:T(8,128)(2,1)S(1)}, bf16[128,512]{1,0:T(8,128)(2,1)S(1)}, u32[]{:S(2)}, u32[]{:S(2)}) collective-permute-start(bf16[128,512]{1,0:T(8,128)(2,1)S(1)} %get-tuple-element.68), channel_id=1, source_target_pairs={{0,4},{4,0},{1,5},{5,1},{2,6},{6,2},{3,7},{7,3},{8,12},{12,8},{9,1... | collective-permute-start | bytes 393224 | tf_op jit(solution)/shard_map/ppermute | solution.py:52
  40.6 14.0 %collective-permute-start.7 = (bf16[128,512]{1,0:T(8,128)(2,1)S(1)}, bf16[128,512]{1,0:T(8,128)(2,1)S(1)}, u32[]{:S(2)}, u32[]{:S(2)}) collective-permute-start(bf16[128,512]{1,0:T(8,128)(2,1)S(1)} %get-tuple-element.69), channel_id=1, source_target_pairs={{0,8},{8,0},{1,9},{9,1},{2,10},{10,2},{3,11},{11,3},{4,12},{12,4},... | collective-permute-start | bytes 393224 | tf_op jit(solution)/shard_map/ppermute | solution.py:52
  42.6 8.4 %collective-permute-start.17 = (bf16[32,512]{1,0:T(8,128)(2,1)S(1)}, bf16[32,512]{1,0:T(8,128)(2,1)S(1)}, u32[]{:S(2)}, u32[]{:S(2)}) collective-permute-start(bf16[32,512]{1,0:T(8,128)(2,1)S(1)} %get-tuple-element.93), channel_id=1, source_target_pairs={{0,8},{8,0},{1,9},{9,1},{2,10},{10,2},{3,11},{11,3},{4,12},{12,4},... | collective-permute-start | bytes 98312 | tf_op jit(solution)/shard_map/ppermute | solution.py:52
  51.0 5.5 %collective-permute-start.18 = (bf16[64,512]{1,0:T(8,128)(2,1)S(1)}, bf16[64,512]{1,0:T(8,128)(2,1)S(1)}, u32[]{:S(2)}, u32[]{:S(2)}) collective-permute-start(bf16[64,512]{1,0:T(8,128)(2,1)S(1)} %shard_map.157.refs_0_), channel_id=1, source_target_pairs={{0,16},{16,0},{1,17},{17,1},{2,18},{18,2},{3,19},{19,3},{4,20},{20... | collective-permute-start | bytes 196616 | tf_op jit(solution)/shard_map/ppermute | solution.py:52
  52.6 4.0 %collective-permute-start.19 = (bf16[32,512]{1,0:T(8,128)(2,1)S(1)}, bf16[32,512]{1,0:T(8,128)(2,1)S(1)}, u32[]{:S(2)}, u32[]{:S(2)}) collective-permute-start(bf16[32,512]{1,0:T(8,128)(2,1)S(1)} %shard_map.163.refs_1_), channel_id=1, source_target_pairs={{0,16},{16,0},{1,17},{17,1},{2,18},{18,2},{3,19},{19,3},{4,20},{20... | collective-permute-start | bytes 98312 | tf_op jit(solution)/shard_map/ppermute | solution.py:52
  (1 other events, 1.4 us)
